TPU v7x, 512 devices: a whole 4x8x8 slice. The times are simulated.
512 devices in a mesh: tm: 64 (over y_hi, z, core), chan: 8 (over y_lo, x).
Axes of the slice: x: 4, y: 8 (y_hi: 4, y_lo: 2; y = y_hi * 2 + y_lo), z: 8, core: 2. Of those that a mesh axis runs over, the one named last changes fastest.
Arguments:
- samples: bfloat16 [32768, 4096], P('tm', 'chan'), may hold values from -6 to 6
- sketch: bfloat16 [4, 4096, 256], P(None, 'chan'), may hold values from -0.046875 to 0.046875
Outputs:
- image: float32 [8, 512, 4, 256], P('chan', 'tm')
All inputs are finite; a program needn't handle non-finite values.
Results may differ from a plain program's by a relative error of at most 0.0029.
Values may be sent and summed in bfloat16 or wider, within the bound.
No kernel may reach another device: no remote copies, remote signals or barrier semaphores. Data moves between devices by JAX's collectives and lax.ppermute only.
A program may use at most 64 MiB of HBM per device.

v0:
```python
import functools

import jax
import jax.numpy as jnp
from jax import lax
from jax.experimental import pallas as pl
from jax.experimental.layout import Layout, with_layout_constraint
from jax.experimental.pallas import tpu as pltpu
from jax.sharding import Mesh
from jax.sharding import PartitionSpec as P


TM = ("y_hi", "z", "core")
CHAN = ("y_lo", "x")
EDGE = 8
LANES = 128
ROOT_SCALE = 512.0
ANY = pl.BlockSpec(memory_space=pl.ANY)
VMEM = pl.BlockSpec(memory_space=pltpu.VMEM)


def local_kernel(kernel, shape, dtype, scratch, in_vmem=True):
    def call(*args):
        if in_vmem:
            args = [pltpu.with_memory_space_constraint(a, pltpu.VMEM) for a in args]
        return pl.pallas_call(
            kernel,
            out_shape=pltpu.VMEM(shape, dtype),
            in_specs=[VMEM if in_vmem else ANY] * len(args),
            out_specs=VMEM,
            scratch_shapes=scratch,
        )(*args)

    return call


def by_rows(array):
    return with_layout_constraint(array, Layout(tuple(range(array.ndim))))


def exchanged(pieces, axis):
    return lax.all_to_all(pieces, axis, split_axis=0, concat_axis=0, tiled=True)


def coded(values):
    root = jnp.sqrt(jnp.abs(values)) * ROOT_SCALE
    return jnp.where(values < 0, -root, root).astype(jnp.float16)


def decoded(codes):
    root = codes.astype(jnp.float32) * (1.0 / ROOT_SCALE)
    return root * jnp.abs(root)


def sketched(samples_hbm, sketch_hbm, out_ref, samples_ref, sketch_ref, held, arrivals):
    blocks = sketch_ref.shape[0]
    rows = samples_ref.shape[0]
    reach, width = out_ref.shape
    own = pltpu.make_async_copy(samples_hbm, samples_ref, arrivals.at[blocks])
    loads = [
        pltpu.make_async_copy(sketch_hbm.at[j], sketch_ref.at[j], arrivals.at[j])
        for j in range(blocks)
    ]
    own.start()
    for load in loads:
        load.start()
    for j in range(blocks):
        held[j, :EDGE] = jnp.zeros((EDGE, width), jnp.float32)
        held[j, EDGE + rows :] = jnp.zeros((held.shape[1] - EDGE - rows, width), jnp.float32)
    own.wait()
    for j in range(blocks):
        loads[j].wait()
        held[j, EDGE : EDGE + rows] = jnp.dot(
            samples_ref[...], sketch_ref[j], preferred_element_type=jnp.float32
        )
    total = held[blocks - 1, EDGE : EDGE + reach]
    for j in range(blocks - 1):
        start = EDGE - (blocks - 1 - j)
        total = total + held[j, start : start + reach]
    out_ref[...] = total


def correlated(block_rows, scale, own_ref, other_ref, tail_ref, sums_ref, out_ref, held, high, low):
    cores, reach, width = sums_ref.shape
    rows = own_ref.shape[1]
    core = lax.axis_index("core")
    mine = pl.ds(pl.multiple_of(core * rows, rows), rows)
    theirs = pl.ds(pl.multiple_of((cores - 1 - core) * rows, rows), rows)
    ends = pl.ds(cores * rows, tail_ref.shape[1])
    depth = cores * rows + 2 * EDGE
    held[:EDGE] = jnp.zeros((EDGE, width), jnp.float32)
    held[EDGE + reach :] = jnp.zeros((held.shape[0] - EDGE - reach, width), jnp.float32)
    held[EDGE : EDGE + reach] = sums_ref[0]
    for k in range(1, cores):
        start = EDGE + k * rows
        held[start : start + reach] = held[start : start + reach] + sums_ref[k]
    for sums in (high, low):
        sums[depth:] = jnp.zeros((sums.shape[0] - depth, sums.shape[1]), jnp.bfloat16)
    for i in range(block_rows):
        wide = held[EDGE - 1 - i : EDGE - 1 - i + depth]
        part = wide.astype(jnp.bfloat16)
        high[:depth, i * width : (i + 1) * width] = part
        low[:depth, i * width : (i + 1) * width] = (wide - part.astype(jnp.float32)).astype(jnp.bfloat16)
    step = 2 * width
    for i in range(0, block_rows * width, step):
        found = jnp.zeros((out_ref.shape[0], step), jnp.float32)
        for turned, where in ((own_ref, mine), (other_ref, theirs), (tail_ref, ends)):
            for sums in (high, low):
                found = found + jnp.dot(
                    turned[...], sums[where, i : i + step], preferred_element_type=jnp.float32
                )
        out_ref[:, i : i + step] = (found * scale).astype(out_ref.dtype)


def shards(samples, sketch):
    rows, local = samples.shape
    blocks, _, width = sketch.shape
    cores = lax.axis_size("core")
    near = lax.axis_size(CHAN)
    groups = lax.axis_size(TM)
    half = width // cores
    part = -(-(rows + blocks - 1) // (near * EDGE)) * EDGE
    reach = near * part
    swap = [(i, cores - 1 - i) for i in range(cores)]
    ahead_route = [(i + cores, i) for i in range(groups - cores)]

    other = by_rows(lax.ppermute(samples, "core", swap))
    partial = local_kernel(
        sketched,
        (reach, width),
        jnp.float32,
        [
            pltpu.VMEM(samples.shape, samples.dtype),
            pltpu.VMEM(sketch.shape, sketch.dtype),
            pltpu.VMEM((blocks, reach + 2 * EDGE, width), jnp.float32),
            pltpu.SemaphoreType.DMA((blocks + 1,)),
        ],
        in_vmem=False,
    )(samples, sketch)
    first = lax.axis_index("core") == 0
    ahead = lax.ppermute(jnp.where(first, samples[:EDGE], other[:EDGE]), TM, ahead_route)
    arrived = exchanged(coded(partial).reshape(near, part, width), CHAN)
    total = coded(decoded(arrived).sum(0))
    copies = [
        jnp.broadcast_to(total[None, :, k * half : (k + 1) * half], (near, part, half))
        for k in range(cores)
    ]
    sums = exchanged(jnp.concatenate(copies, 0), ("core", *CHAN))
    tail = jnp.pad(ahead, ((0, LANES - EDGE), (0, 0)))
    scale = 1.0 / (rows * groups) ** 0.5
    found = local_kernel(
        functools.partial(correlated, blocks, scale),
        (local, blocks * half),
        jnp.bfloat16,
        [
            pltpu.VMEM((EDGE + (cores - 1) * rows + reach + 2 * EDGE, half), jnp.float32),
            pltpu.VMEM((cores * rows + LANES, blocks * half), jnp.bfloat16),
            pltpu.VMEM((cores * rows + LANES, blocks * half), jnp.bfloat16),
        ],
    )(samples.T, other.T, tail.T, decoded(sums).reshape(cores, reach, half))
    landed = exchanged(found.reshape(groups, local // groups, blocks * half), TM)
    landed = landed.reshape(groups // cores, cores, local // groups, blocks, half)
    mine = landed.astype(jnp.float32).sum(0)
    return jnp.concatenate([mine[k] for k in range(cores)], -1)[None]


def solution(mesh):
    sizes = {"y_hi": 4, "z": 8, "core": 2, "y_lo": 2, "x": 4}
    fine = Mesh(mesh.devices.reshape(tuple(sizes.values())), tuple(sizes))
    placed = (P(TM, CHAN), P(None, CHAN, None))
    return jax.shard_map(
        shards, mesh=fine, in_specs=placed, out_specs=P(CHAN, TM, None, None), check_vma=False
    )
```

profile of v0, /device:TPU:1, one launch (start us, length us, event | category | flops | bytes accessed | tf_op | source)
XLA Modules:
  0.0 73.4 jit_solution(16065124047351127808)
XLA Ops:
  0.0 2.8 %shard_map.28 = f32[576,256]{1,0:T(8,128)S(1)} custom-call(bf16[512,512]{1,0:T(8,128)(2,1)} %samples_hbm.1, bf16[4,512,256]{2,1,0:T(8,128)(2,1)} %sketch_hbm.1), custom_call_target="tpu_custom_call" | custom-call | tf_op jit(solution)/shard_map/pallas_call | solution.py:26
  2.9 0.0 copy-start
  2.9 1.0 %fusion = f16[576,256]{1,0:T(8,128)(2,1)} fusion(f32[576,256]{1,0:T(8,128)S(1)} %shard_map.28), kind=kLoop, calls=%fused_computation.4 | loop fusion | flops 884736 | bytes 884736 | tf_op jit(solution)/shard_map/convert_element_type | solution.py:47
  3.8 5.8 %all-to-all-start = ((f16[8,72,256]{2,1,0:T(8,128)(2,1)}), f16[8,72,256]{2,1,0:T(8,128)(2,1)S(1)}, u32[]{:S(2)}, u32[]{:S(2)}) async-start(f16[8,72,256]{2,1,0:T(8,128)(2,1)} %bitcast.3), calls=%async_computation | async-start | bytes 589824 | tf_op jit(solution)/shard_map/all_to_all | solution.py:42
  9.7 0.0 copy-done
  9.7 6.3 %collective-permute-start = (bf16[512,512]{1,0:T(8,128)(2,1)S(1)}, bf16[512,512]{1,0:T(8,128)(2,1)S(1)}, u32[]{:S(2)}, u32[]{:S(2)}) collective-permute-start(bf16[512,512]{1,0:T(8,128)(2,1)S(1)} %copy-done), channel_id=1, source_target_pairs={{0,8},{8,0},{1,9},{9,1},{2,10},{10,2},{3,11},{11,3},{4,12},{12,4},... | collective-permute-start | bytes 1572872 | tf_op jit(solution)/shard_map/ppermute | solution.py:127
  16.0 0.0 all-to-all-done
  16.0 0.1 fusion.1
  16.3 0.8 %pad_maximum_fusion = f16[16,72,128]{2,1,0:T(8,128)(2,1)} fusion(f16[8,72,128]{2,1,0:T(8,128)(2,1)S(1)} %broadcast_in_dim.7, f16[8,72,128]{2,1,0:T(8,128)(2,1)S(1)} %broadcast_in_dim.6), kind=kLoop, calls=%fused_computation.6 | loop fusion | flops 147456 | bytes 589824 | tf_op jit(solution)/shard_map/concatenate | solution.py:148
  17.1 8.7 %all-to-all-start.1 = ((f16[16,72,128]{2,1,0:T(8,128)(2,1)}), f16[16,72,128]{2,1,0:T(8,128)(2,1)S(1)}, u32[]{:S(2)}, u32[]{:S(2)}) async-start(f16[16,72,128]{2,1,0:T(8,128)(2,1)} %pad_maximum_fusion), calls=%async_computation.1 | async-start | bytes 589824 | tf_op jit(solution)/shard_map/all_to_all | solution.py:42
  25.8 0.2 copy.9
  26.0 0.0 collective-permute-done
  26.0 0.2 copy.10
  26.2 1.3 %collective-permute-start.1 = (bf16[8,512]{0,1:T(8,128)(2,1)S(1)}, bf16[8,512]{0,1:T(8,128)(2,1)S(1)}, u32[]{:S(2)}, u32[]{:S(2)}) collective-permute-start(bf16[8,512]{0,1:T(8,128)(2,1)S(1)} %broadcast_select_fusion), channel_id=1, source_target_pairs={{16,0},{24,8},{32,16},{40,24},{48,32},{56,40},{64,48},{72,56},{80,... | collective-permute-start | bytes 24584 | tf_op jit(solution)/shard_map/ppermute | solution.py:141
  27.5 0.2 copy.7
  27.7 0.2 copy.8
  27.9 5.0 %collective-permute-done.1 = bf16[8,512]{0,1:T(8,128)(2,1)S(1)} collective-permute-done((bf16[8,512]{0,1:T(8,128)(2,1)S(1)}, bf16[8,512]{0,1:T(8,128)(2,1)S(1)}, u32[]{:S(2)}, u32[]{:S(2)}) %collective-permute-start.1) | collective-permute-done | bytes 8224 | tf_op jit(solution)/shard_map/ppermute | solution.py:141
  33.0 0.9 %all-to-all-done.1 = f16[16,72,128]{2,1,0:T(8,128)(2,1)S(1)} async-done(((f16[16,72,128]{2,1,0:T(8,128)(2,1)}), f16[16,72,128]{2,1,0:T(8,128)(2,1)S(1)}, u32[]{:S(2)}, u32[]{:S(2)}) %all-to-all-start.1) | async-done | bytes 294944 | tf_op jit(solution)/shard_map/all_to_all | solution.py:42
  33.9 0.1 abs_multiply_fusion
  34.0 2.0 %shard_map.29 = bf16[512,512]{1,0:T(8,128)(2,1)S(1)} custom-call(bf16[512,512]{1,0:T(8,128)(2,1)S(1)} %bitcast.16, bf16[512,512]{1,0:T(8,128)(2,1)S(1)} %bitcast.17, bf16[512,128]{1,0:T(8,128)(2,1)S(1)} %pad_bitcast_fusion.tail_ref, f32[2,576,128]{2,1,0:T(8,128)S(1)} %bitcast.15), custom_call_target="tpu_custom_call" | custom-call | tf_op jit(solution)/shard_map/pallas_call | solution.py:26
  35.9 36.7 %all_to_all.15 = bf16[64,8,512]{2,1,0:T(8,128)(2,1)S(1)} all-to-all(bf16[64,8,512]{2,1,0:T(8,128)(2,1)S(1)} %bitcast.18), channel_id=1, replica_groups=mesh['y_hi'=4,'z'=8,'core'=2,'y_lo'=2,'x'=4] {'y_hi','z','core'}, dimensions={0} | all-to-all | bytes 1048576 | tf_op jit(solution)/shard_map/all_to_all | solution.py:42
  72.7 0.1 convert_reduce_fusion
  72.8 0.6 copy.11
  (10 shorter events, 0.2 us)
Async XLA Ops:
  2.9 6.8 %copy-start = (bf16[512,512]{1,0:T(8,128)(2,1)S(1)}, bf16[512,512]{1,0:T(8,128)(2,1)}, u32[]{:S(2)}) copy-start(bf16[512,512]{1,0:T(8,128)(2,1)} %samples_hbm.1) | copy-start | bytes 1572868
  3.8 12.2 %all-to-all-start = ((f16[8,72,256]{2,1,0:T(8,128)(2,1)}), f16[8,72,256]{2,1,0:T(8,128)(2,1)S(1)}, u32[]{:S(2)}, u32[]{:S(2)}) async-start(f16[8,72,256]{2,1,0:T(8,128)(2,1)} %bitcast.3), calls=%async_computation | async-start | bytes 589824 | tf_op jit(solution)/shard_map/all_to_all | solution.py:42
  9.7 16.3 %collective-permute-start = (bf16[512,512]{1,0:T(8,128)(2,1)S(1)}, bf16[512,512]{1,0:T(8,128)(2,1)S(1)}, u32[]{:S(2)}, u32[]{:S(2)}) collective-permute-start(bf16[512,512]{1,0:T(8,128)(2,1)S(1)} %copy-done), channel_id=1, source_target_pairs={{0,8},{8,0},{1,9},{9,1},{2,10},{10,2},{3,11},{11,3},{4,12},{12,4},... | collective-permute-start | bytes 1572872 | tf_op jit(solution)/shard_map/ppermute | solution.py:127
  17.1 16.8 %all-to-all-start.1 = ((f16[16,72,128]{2,1,0:T(8,128)(2,1)}), f16[16,72,128]{2,1,0:T(8,128)(2,1)S(1)}, u32[]{:S(2)}, u32[]{:S(2)}) async-start(f16[16,72,128]{2,1,0:T(8,128)(2,1)} %pad_maximum_fusion), calls=%async_computation.1 | async-start | bytes 589824 | tf_op jit(solution)/shard_map/all_to_all | solution.py:42
  26.2 6.8 %collective-permute-start.1 = (bf16[8,512]{0,1:T(8,128)(2,1)S(1)}, bf16[8,512]{0,1:T(8,128)(2,1)S(1)}, u32[]{:S(2)}, u32[]{:S(2)}) collective-permute-start(bf16[8,512]{0,1:T(8,128)(2,1)S(1)} %broadcast_select_fusion), channel_id=1, source_target_pairs={{16,0},{24,8},{32,16},{40,24},{48,32},{56,40},{64,48},{72,56},{80,... | collective-permute-start | bytes 24584 | tf_op jit(solution)/shard_map/ppermute | solution.py:141
where the time goes:
time: 73.8 us; the launch traced here: 73.4 us
  blocking collectives  36.7 us (50%)
  starting transfers between devices  22.2 us (30%)
  waiting for transfers between devices  5.96 us (8%)
  Pallas kernels  4.8 us (7%)
  other arithmetic  2.09 us (3%)
  local copies, waits for them, and re-layouts  1.47 us (2%)
    all_to_all x1, blocking collectives, exchanged(): return lax.all_to_all(pieces, axis, split_axis=0, concat_axis=0, tiled=True)  36.7 us
    all_to_all x2, starting transfers between devices, exchanged(): return lax.all_to_all(pieces, axis, split_axis=0, concat_axis=0, tiled=True)  14.6 us
    ppermute x1, starting transfers between devices, shards(): other = by_rows(lax.ppermute(samples, 'core', swap))  6.33 us
    ppermute x1, waiting for transfers between devices, shards(): lax.ppermute(jnp.where(first, samples[:EDGE], other[:EDGE]), TM, ahead_ro...  5.04 us
    pallas_call x2, Pallas kernels, call(): pl.pallas_call(kernel, out_shape=pltpu.VMEM(shape, dtype), in_specs=[VMEM...  4.8 us
  transfers between devices with their start and end apart: 4, of which 2 were waited for; matrix products, arithmetic and copies ran while one was open for 2% of the time, Pallas kernels for 0%

commit v1 on v0

v1 whole, which is shorter than its diff:
```python
import functools

import jax
import jax.numpy as jnp
from jax import lax
from jax.experimental import pallas as pl
from jax.experimental.layout import Layout, with_layout_constraint
from jax.experimental.pallas import tpu as pltpu
from jax.sharding import Mesh
from jax.sharding import PartitionSpec as P


TM = ("y_hi", "z", "core")
CHAN = ("y_lo", "x")
EDGE = 8
LANES = 128
ROOT_SCALE = 512.0
ANY = pl.BlockSpec(memory_space=pl.ANY)
VMEM = pl.BlockSpec(memory_space=pltpu.VMEM)


def local_kernel(kernel, out_shapes, scratch, in_vmem=True):
    def call(*args):
        if in_vmem:
            args = [pltpu.with_memory_space_constraint(a, pltpu.VMEM) for a in args]
        return pl.pallas_call(
            kernel,
            out_shape=[pltpu.VMEM(shape, dtype) for shape, dtype in out_shapes],
            in_specs=[VMEM if in_vmem else ANY] * len(args),
            out_specs=[VMEM] * len(out_shapes),
            scratch_shapes=scratch,
        )(*args)

    return call


def by_rows(array):
    return with_layout_constraint(array, Layout(tuple(range(array.ndim))))


def exchanged(pieces, axis):
    return lax.all_to_all(pieces, axis, split_axis=0, concat_axis=0, tiled=True)


def coded(values):
    root = jnp.sqrt(jnp.abs(values)) * ROOT_SCALE
    return jnp.where(values < 0, -root, root).astype(jnp.float16)


def decoded(codes):
    root = codes.astype(jnp.float32) * (1.0 / ROOT_SCALE)
    return root * jnp.abs(root)


def shifted_sum(held, reach, width):
    blocks = held.shape[1] // width
    total = held[EDGE : EDGE + reach, (blocks - 1) * width :]
    for j in range(blocks - 1):
        start = EDGE - (blocks - 1 - j)
        total = total + held[start : start + reach, j * width : (j + 1) * width]
    return total


def clear_edges(held, rows):
    held[:EDGE] = jnp.zeros((EDGE, held.shape[1]), jnp.float32)
    held[EDGE + rows :] = jnp.zeros((held.shape[0] - EDGE - rows, held.shape[1]), jnp.float32)


def sketched_own(samples_hbm, sketch_hbm, own_ref, columns_ref, samples_ref, held, arrivals):
    blocks = sketch_hbm.shape[0]
    rows = samples_ref.shape[0]
    reach, width = own_ref.shape
    start = pl.multiple_of(lax.axis_index("core") * width, width)
    rows_load = pltpu.make_async_copy(samples_hbm, samples_ref, arrivals.at[blocks])
    loads = [
        pltpu.make_async_copy(
            sketch_hbm.at[j, :, pl.ds(start, width)],
            columns_ref.at[:, j * width : (j + 1) * width],
            arrivals.at[j],
        )
        for j in range(blocks)
    ]
    rows_load.start()
    for load in loads:
        load.start()
    clear_edges(held, rows)
    rows_load.wait()
    for j in range(0, blocks, 2):
        pair = slice(j * width, (j + 2) * width)
        for load in loads[j : j + 2]:
            load.wait()
        held[EDGE : EDGE + rows, pair] = jnp.dot(
            samples_ref[...], columns_ref[:, pair], preferred_element_type=jnp.float32
        )
    own_ref[...] = shifted_sum(held, reach, width)


def sketched_chip(other_ref, columns_ref, own_ref, out_ref, held):
    rows = other_ref.shape[0]
    reach, width = own_ref.shape
    cores = (out_ref.shape[0] - EDGE) // rows
    clear_edges(held, rows)
    held[EDGE : EDGE + rows] = jnp.dot(
        other_ref[...], columns_ref[...], preferred_element_type=jnp.float32
    )
    core = lax.axis_index("core")
    mine = pl.ds(pl.multiple_of(core * rows, rows), reach)
    theirs = pl.ds(pl.multiple_of((cores - 1 - core) * rows, rows), reach)
    out_ref[...] = jnp.zeros_like(out_ref)
    out_ref[mine] = own_ref[...]
    out_ref[theirs] = out_ref[theirs] + shifted_sum(held, reach, width)


def correlated(block_rows, scale, own_ref, other_ref, tail_ref, sums_ref, out_ref, held, high, low):
    reach, width = sums_ref.shape
    rows = own_ref.shape[1]
    cores = reach // rows
    core = lax.axis_index("core")
    mine = pl.ds(pl.multiple_of(core * rows, rows), rows)
    theirs = pl.ds(pl.multiple_of((cores - 1 - core) * rows, rows), rows)
    ends = pl.ds(cores * rows, tail_ref.shape[1])
    depth = cores * rows + 2 * EDGE
    held[:EDGE] = jnp.zeros((EDGE, width), jnp.float32)
    held[EDGE:] = sums_ref[...]
    for sums in (high, low):
        sums[depth:] = jnp.zeros((sums.shape[0] - depth, sums.shape[1]), jnp.bfloat16)
    for i in range(block_rows):
        wide = held[EDGE - 1 - i : EDGE - 1 - i + depth]
        part = wide.astype(jnp.bfloat16)
        high[:depth, i * width : (i + 1) * width] = part
        low[:depth, i * width : (i + 1) * width] = (wide - part.astype(jnp.float32)).astype(jnp.bfloat16)
    step = 2 * width
    for i in range(0, block_rows * width, step):
        found = jnp.zeros((out_ref.shape[0], step), jnp.float32)
        for turned, where in ((own_ref, mine), (other_ref, theirs), (tail_ref, ends)):
            for sums in (high, low):
                found = found + jnp.dot(
                    turned[...], sums[where, i : i + step], preferred_element_type=jnp.float32
                )
        out_ref[:, i : i + step] = (found * scale).astype(out_ref.dtype)


def shards(samples, sketch):
    rows, local = samples.shape
    blocks, _, width = sketch.shape
    cores = lax.axis_size("core")
    near = lax.axis_size(CHAN)
    groups = lax.axis_size(TM)
    half = width // cores
    part = -(-(cores * rows + blocks - 1) // (near * EDGE)) * EDGE
    reach = near * part
    swap = [(i, cores - 1 - i) for i in range(cores)]
    ahead_route = [(i + cores, i) for i in range(groups - cores)]

    other = by_rows(lax.ppermute(samples, "core", swap))
    held = pltpu.VMEM((rows + 3 * EDGE, blocks * half), jnp.float32)
    own, columns = local_kernel(
        sketched_own,
        [((rows + EDGE, half), jnp.float32), ((local, blocks * half), sketch.dtype)],
        [pltpu.VMEM(samples.shape, samples.dtype), held, pltpu.SemaphoreType.DMA((blocks + 1,))],
        in_vmem=False,
    )(samples, sketch)
    (partial,) = local_kernel(
        sketched_chip, [((reach, half), jnp.float32)], [held]
    )(other, columns, own)
    first = lax.axis_index("core") == 0
    ahead = lax.ppermute(jnp.where(first, samples[:EDGE], other[:EDGE]), TM, ahead_route)
    arrived = exchanged(coded(partial).reshape(near, part, half), CHAN)
    total = coded(decoded(arrived).sum(0))
    sums = exchanged(jnp.broadcast_to(total[None], (near, part, half)), CHAN)
    tail = jnp.pad(ahead, ((0, LANES - EDGE), (0, 0)))
    scale = 1.0 / (rows * groups) ** 0.5
    steps = pltpu.VMEM((cores * rows + LANES, blocks * half), jnp.bfloat16)
    (found,) = local_kernel(
        functools.partial(correlated, blocks, scale),
        [((local, blocks * half), jnp.bfloat16)],
        [pltpu.VMEM((EDGE + reach, half), jnp.float32), steps, steps],
    )(samples.T, other.T, tail.T, decoded(sums).reshape(reach, half))
    landed = exchanged(found.reshape(groups, local // groups, blocks * half), TM)
    landed = landed.reshape(groups // cores, cores, local // groups, blocks, half)
    mine = landed.astype(jnp.float32).sum(0)
    return jnp.concatenate([mine[k] for k in range(cores)], -1)[None]


def solution(mesh):
    sizes = {"y_hi": 4, "z": 8, "core": 2, "y_lo": 2, "x": 4}
    fine = Mesh(mesh.devices.reshape(tuple(sizes.values())), tuple(sizes))
    placed = (P(TM, CHAN), P(None, CHAN, None))
    return jax.shard_map(
        shards, mesh=fine, in_specs=placed, out_specs=P(CHAN, TM, None, None), check_vma=False
    )
```

time: 73.8 us -> 74.4 us (level)
  blocking collectives: 36.7 us -> 49.1 us
  starting transfers between devices: 22.2 us -> 13.4 us
  waiting for transfers between devices: 5.96 us -> 4.28 us
  other arithmetic: 2.09 us -> 0.58 us
    all_to_all x1 -> x2, blocking collectives: 36.7 us -> 49.1 us  [exchanged(): return lax.all_to_all(pieces, axis, split_axis=0, concat_axis=0, tiled=True)]
    all_to_all x2 -> x1, starting transfers between devices: 14.6 us -> 3.42 us  [exchanged(): return lax.all_to_all(pieces, axis, split_axis=0, concat_axis=0, tiled=True)]
    ppermute x1, starting transfers between devices: 6.33 us -> 8.74 us  [shards(): other = by_rows(lax.ppermute(samples, 'core', swap))]
    all_to_all x2 -> x1, waiting for transfers between devices: 0.92 us -> 0.01 us  [exchanged(): return lax.all_to_all(pieces, axis, split_axis=0, concat_axis=0, tiled=True)]
    concatenate x1 -> x0, other arithmetic: 0.79 us -> none  [shards(): sums = exchanged(jnp.concatenate(copies, 0), ('core', *CHAN))]
    ppermute x1, waiting for transfers between devices: 5.04 us -> 4.27 us  [shards(): lax.ppermute(jnp.where(first, samples[:EDGE], other[:EDGE]), TM, ahead_ro...]
    pallas_call x2 -> x3, Pallas kernels: 4.8 us -> 4.33 us  [call(): pl.pallas_call(kernel, out_shape=[pltpu.VMEM(shape, dtype) for shape, dty...]
  transfers between devices with their start and end apart: 4 -> 3, of which waited for: 2 -> 1; matrix products, arithmetic and copies ran while one was open for 2% -> 1% of each run, Pallas kernels for 0% -> 3%
where the time goes in v1:
time: 74.4 us; the launch traced here: 74.1 us
  blocking collectives  49.1 us (66%)
  starting transfers between devices  13.4 us (18%)
  Pallas kernels  4.33 us (6%)
  waiting for transfers between devices  4.28 us (6%)
  local copies, waits for them, and re-layouts  2.15 us (3%)
    all_to_all x2, blocking collectives, exchanged(): return lax.all_to_all(pieces, axis, split_axis=0, concat_axis=0, tiled=True)  49.1 us
    ppermute x1, starting transfers between devices, shards(): other = by_rows(lax.ppermute(samples, 'core', swap))  8.74 us
    pallas_call x3, Pallas kernels, call(): pl.pallas_call(kernel, out_shape=[pltpu.VMEM(shape, dtype) for shape, dty...  4.33 us
    ppermute x1, waiting for transfers between devices, shards(): lax.ppermute(jnp.where(first, samples[:EDGE], other[:EDGE]), TM, ahead_ro...  4.27 us
    all_to_all x1, starting transfers between devices, exchanged(): return lax.all_to_all(pieces, axis, split_axis=0, concat_axis=0, tiled=True)  3.42 us
  transfers between devices with their start and end apart: 3, of which 1 were waited for; matrix products, arithmetic and copies ran while one was open for 1% of the time, Pallas kernels for 3%

profile of v1, /device:TPU:1, one launch (start us, length us, event | category | flops | bytes accessed | tf_op | source)
XLA Modules:
  0.0 74.1 jit_solution(13670879147183778505)
XLA Ops:
  0.0 8.7 %collective-permute-start = (bf16[512,512]{1,0:T(8,128)(2,1)}, bf16[512,512]{1,0:T(8,128)(2,1)S(1)}, u32[]{:S(2)}, u32[]{:S(2)}) collective-permute-start(bf16[512,512]{1,0:T(8,128)(2,1)} %samples_hbm.1), channel_id=1, source_target_pairs={{0,8},{8,0},{1,9},{9,1},{2,10},{10,2},{3,11},{11,3},{4,12},{12,4},... | collective-permute-start | bytes 1572872 | tf_op jit(solution)/shard_map/ppermute | solution.py:155
  8.7 2.0 %shard_map.28 = (f32[520,128]{1,0:T(8,128)S(1)}, bf16[512,512]{1,0:T(8,128)(2,1)S(1)}) custom-call(bf16[512,512]{1,0:T(8,128)(2,1)} %samples_hbm.1, bf16[4,512,256]{2,1,0:T(8,128)(2,1)} %sketch_hbm.1), custom_call_target="tpu_custom_call" | custom-call | tf_op jit(solution)/shard_map/pallas_call | solution.py:26
  10.8 0.0 collective-permute-done.other_ref
  10.8 0.4 shard_map.29
  11.2 0.3 fusion
  11.5 9.8 %all_to_all.15 = f16[8,136,128]{2,1,0:T(8,128)(2,1)S(1)} all-to-all(f16[8,136,128]{2,1,0:T(8,128)(2,1)S(1)} %bitcast.20), channel_id=1, replica_groups=mesh['y_hi'=4,'z'=8,'core'=2,'y_lo'=2,'x'=4] {'y_lo','x'}, dimensions={0} | all-to-all | bytes 557056 | tf_op jit(solution)/shard_map/all_to_all | solution.py:42
  21.3 0.1 fusion.1
  21.4 0.0 copy-start
  21.5 0.7 broadcast_in_dim.4
  22.2 3.4 %all-to-all-start.1 = ((f16[8,136,128]{2,1,0:T(8,128)(2,1)}), f16[8,136,128]{2,1,0:T(8,128)(2,1)S(1)}, u32[]{:S(2)}, u32[]{:S(2)}) async-start(f16[8,136,128]{2,1,0:T(8,128)(2,1)} %broadcast_in_dim.4), calls=%async_computation.1 | async-start | bytes 557056 | tf_op jit(solution)/shard_map/all_to_all | solution.py:42
  25.6 0.0 copy-done
  25.7 0.2 copy.9
  25.8 0.2 copy.10
  26.0 1.3 %collective-permute-start.1 = (bf16[8,512]{0,1:T(8,128)(2,1)S(1)}, bf16[8,512]{0,1:T(8,128)(2,1)S(1)}, u32[]{:S(2)}, u32[]{:S(2)}) collective-permute-start(bf16[8,512]{0,1:T(8,128)(2,1)S(1)} %broadcast_select_fusion), channel_id=1, source_target_pairs={{16,0},{24,8},{32,16},{40,24},{48,32},{56,40},{64,48},{72,56},{80,... | collective-permute-start | bytes 24584 | tf_op jit(solution)/shard_map/ppermute | solution.py:167
  27.3 0.2 copy.7
  27.6 0.2 copy.8
  27.8 4.3 %collective-permute-done.1 = bf16[8,512]{0,1:T(8,128)(2,1)S(1)} collective-permute-done((bf16[8,512]{0,1:T(8,128)(2,1)S(1)}, bf16[8,512]{0,1:T(8,128)(2,1)S(1)}, u32[]{:S(2)}, u32[]{:S(2)}) %collective-permute-start.1) | collective-permute-done | bytes 8224 | tf_op jit(solution)/shard_map/ppermute | solution.py:167
  32.1 0.0 all-to-all-done.1
  32.1 0.1 abs_multiply_fusion
  32.2 1.9 %shard_map.30 = bf16[512,512]{1,0:T(8,128)(2,1)S(1)} custom-call(bf16[512,512]{1,0:T(8,128)(2,1)S(1)} %bitcast.16, bf16[512,512]{1,0:T(8,128)(2,1)S(1)} %bitcast.17, bf16[512,128]{1,0:T(8,128)(2,1)S(1)} %pad_bitcast_fusion.tail_ref, f32[1088,128]{1,0:T(8,128)S(1)} %bitcast.15), custom_call_target="tpu_custom_call" | custom-call | tf_op jit(solution)/shard_map/pallas_call | solution.py:26
  34.1 39.3 %all_to_all.16 = bf16[64,8,512]{2,1,0:T(8,128)(2,1)S(1)} all-to-all(bf16[64,8,512]{2,1,0:T(8,128)(2,1)S(1)} %bitcast.18), channel_id=1, replica_groups=mesh['y_hi'=4,'z'=8,'core'=2,'y_lo'=2,'x'=4] {'y_hi','z','core'}, dimensions={0} | all-to-all | bytes 1048576 | tf_op jit(solution)/shard_map/all_to_all | solution.py:42
  73.3 0.1 convert_reduce_fusion
  73.4 0.6 copy.11
  (7 shorter events, 0.1 us)
Async XLA Ops:
  0.0 10.8 %collective-permute-start = (bf16[512,512]{1,0:T(8,128)(2,1)}, bf16[512,512]{1,0:T(8,128)(2,1)S(1)}, u32[]{:S(2)}, u32[]{:S(2)}) collective-permute-start(bf16[512,512]{1,0:T(8,128)(2,1)} %samples_hbm.1), channel_id=1, source_target_pairs={{0,8},{8,0},{1,9},{9,1},{2,10},{10,2},{3,11},{11,3},{4,12},{12,4},... | collective-permute-start | bytes 1572872 | tf_op jit(solution)/shard_map/ppermute | solution.py:155
  21.4 4.2 %copy-start = (bf16[512,512]{1,0:T(8,128)(2,1)S(1)}, bf16[512,512]{1,0:T(8,128)(2,1)}, u32[]{:S(2)}) copy-start(bf16[512,512]{1,0:T(8,128)(2,1)} %samples_hbm.1) | copy-start | bytes 1572868
  22.2 9.9 %all-to-all-start.1 = ((f16[8,136,128]{2,1,0:T(8,128)(2,1)}), f16[8,136,128]{2,1,0:T(8,128)(2,1)S(1)}, u32[]{:S(2)}, u32[]{:S(2)}) async-start(f16[8,136,128]{2,1,0:T(8,128)(2,1)} %broadcast_in_dim.4), calls=%async_computation.1 | async-start | bytes 557056 | tf_op jit(solution)/shard_map/all_to_all | solution.py:42
  26.0 6.0 %collective-permute-start.1 = (bf16[8,512]{0,1:T(8,128)(2,1)S(1)}, bf16[8,512]{0,1:T(8,128)(2,1)S(1)}, u32[]{:S(2)}, u32[]{:S(2)}) collective-permute-start(bf16[8,512]{0,1:T(8,128)(2,1)S(1)} %broadcast_select_fusion), channel_id=1, source_target_pairs={{16,0},{24,8},{32,16},{40,24},{48,32},{56,40},{64,48},{72,56},{80,... | collective-permute-start | bytes 24584 | tf_op jit(solution)/shard_map/ppermute | solution.py:167

commit v2 on v1

--- a/solution.py
+++ b/solution.py
@@ -14,7 +14,8 @@
 CHAN = ("y_lo", "x")
 EDGE = 8
 LANES = 128
-ROOT_SCALE = 512.0
+SKETCH_ROOT = 512.0
+IMAGE_ROOT = 128.0
 ANY = pl.BlockSpec(memory_space=pl.ANY)
 VMEM = pl.BlockSpec(memory_space=pltpu.VMEM)
 
@@ -42,13 +43,13 @@
     return lax.all_to_all(pieces, axis, split_axis=0, concat_axis=0, tiled=True)
 
 
-def coded(values):
-    root = jnp.sqrt(jnp.abs(values)) * ROOT_SCALE
+def coded(values, root_scale):
+    root = jnp.sqrt(jnp.abs(values)) * root_scale
     return jnp.where(values < 0, -root, root).astype(jnp.float16)
 
 
-def decoded(codes):
-    root = codes.astype(jnp.float32) * (1.0 / ROOT_SCALE)
+def decoded(codes, root_scale):
+    root = codes.astype(jnp.float32) * (1.0 / root_scale)
     return root * jnp.abs(root)
 
 
@@ -111,7 +112,7 @@
     out_ref[theirs] = out_ref[theirs] + shifted_sum(held, reach, width)
 
 
-def correlated(block_rows, scale, own_ref, other_ref, tail_ref, sums_ref, out_ref, held, high, low):
+def correlated(block_rows, scale, own_ref, other_ref, tail_ref, sums_ref, out_ref, held, steps):
     reach, width = sums_ref.shape
     rows = own_ref.shape[1]
     cores = reach // rows
@@ -122,22 +123,18 @@
     depth = cores * rows + 2 * EDGE
     held[:EDGE] = jnp.zeros((EDGE, width), jnp.float32)
     held[EDGE:] = sums_ref[...]
-    for sums in (high, low):
-        sums[depth:] = jnp.zeros((sums.shape[0] - depth, sums.shape[1]), jnp.bfloat16)
+    steps[depth:] = jnp.zeros((steps.shape[0] - depth, steps.shape[1]), steps.dtype)
     for i in range(block_rows):
-        wide = held[EDGE - 1 - i : EDGE - 1 - i + depth]
-        part = wide.astype(jnp.bfloat16)
-        high[:depth, i * width : (i + 1) * width] = part
-        low[:depth, i * width : (i + 1) * width] = (wide - part.astype(jnp.float32)).astype(jnp.bfloat16)
-    step = 2 * width
-    for i in range(0, block_rows * width, step):
-        found = jnp.zeros((out_ref.shape[0], step), jnp.float32)
+        moved = held[EDGE - 1 - i : EDGE - 1 - i + depth]
+        steps[:depth, i * width : (i + 1) * width] = moved.astype(steps.dtype)
+    wide = 2 * width
+    for i in range(0, block_rows * width, wide):
+        found = jnp.zeros((out_ref.shape[0], wide), jnp.float32)
         for turned, where in ((own_ref, mine), (other_ref, theirs), (tail_ref, ends)):
-            for sums in (high, low):
-                found = found + jnp.dot(
-                    turned[...], sums[where, i : i + step], preferred_element_type=jnp.float32
-                )
-        out_ref[:, i : i + step] = (found * scale).astype(out_ref.dtype)
+            found = found + jnp.dot(
+                turned[...], steps[where, i : i + wide], preferred_element_type=jnp.float32
+            )
+        out_ref[:, i : i + wide] = found * scale
 
 
 def shards(samples, sketch):
@@ -165,20 +162,25 @@
     )(other, columns, own)
     first = lax.axis_index("core") == 0
     ahead = lax.ppermute(jnp.where(first, samples[:EDGE], other[:EDGE]), TM, ahead_route)
-    arrived = exchanged(coded(partial).reshape(near, part, half), CHAN)
-    total = coded(decoded(arrived).sum(0))
+    arrived = exchanged(coded(partial, SKETCH_ROOT).reshape(near, part, half), CHAN)
+    total = decoded(arrived, SKETCH_ROOT).sum(0).astype(jnp.bfloat16)
+    total, *turned = lax.optimization_barrier((total, samples.T, other.T))
+    tail = jnp.pad(ahead, ((0, LANES - EDGE), (0, 0)))
     sums = exchanged(jnp.broadcast_to(total[None], (near, part, half)), CHAN)
-    tail = jnp.pad(ahead, ((0, LANES - EDGE), (0, 0)))
+    sums = sums.astype(jnp.float32).reshape(reach, half)
     scale = 1.0 / (rows * groups) ** 0.5
-    steps = pltpu.VMEM((cores * rows + LANES, blocks * half), jnp.bfloat16)
     (found,) = local_kernel(
         functools.partial(correlated, blocks, scale),
-        [((local, blocks * half), jnp.bfloat16)],
-        [pltpu.VMEM((EDGE + reach, half), jnp.float32), steps, steps],
-    )(samples.T, other.T, tail.T, decoded(sums).reshape(reach, half))
-    landed = exchanged(found.reshape(groups, local // groups, blocks * half), TM)
+        [((local, blocks * half), jnp.float32)],
+        [
+            pltpu.VMEM((EDGE + reach, half), jnp.float32),
+            pltpu.VMEM((cores * rows + LANES, blocks * half), jnp.bfloat16),
+        ],
+    )(*turned, tail.T, sums)
+    pieces = coded(found, IMAGE_ROOT).reshape(groups, local // groups, blocks * half)
+    landed = exchanged(pieces, TM)
     landed = landed.reshape(groups // cores, cores, local // groups, blocks, half)
-    mine = landed.astype(jnp.float32).sum(0)
+    mine = decoded(landed, IMAGE_ROOT).sum(0)
     return jnp.concatenate([mine[k] for k in range(cores)], -1)[None]
 
 

time: 74.4 us -> 74.7 us (level)
  blocking collectives: 49.1 us -> 38.6 us
  waiting for transfers between devices: 4.28 us -> 11 us
  starting transfers between devices: 13.4 us -> 17.1 us
  other arithmetic: 0.58 us -> 1.85 us
  Pallas kernels: 4.33 us -> 3.58 us
    all_to_all x2 -> x1, blocking collectives: 49.1 us -> 38.6 us  [exchanged(): return lax.all_to_all(pieces, axis, split_axis=0, concat_axis=0, tiled=True)]
    all_to_all x1 -> x2, waiting for transfers between devices: 0.01 us -> 6.25 us  [exchanged(): return lax.all_to_all(pieces, axis, split_axis=0, concat_axis=0, tiled=True)]
    all_to_all x1 -> x2, starting transfers between devices: 3.42 us -> 7.04 us  [exchanged(): return lax.all_to_all(pieces, axis, split_axis=0, concat_axis=0, tiled=True)]
    pallas_call x3, Pallas kernels: 4.33 us -> 3.58 us  [call(): pl.pallas_call(kernel, out_shape=[pltpu.VMEM(shape, dtype) for shape, dty...]
  transfers between devices with their start and end apart: 3 -> 4, of which waited for: 1 -> 2; matrix products, arithmetic and copies ran while one was open for 1% -> 1% of each run, Pallas kernels for 3% -> 3%
where the time goes in v2:
time: 74.7 us; the launch traced here: 74.3 us
  blocking collectives  38.6 us (52%)
  starting transfers between devices  17.1 us (23%)
  waiting for transfers between devices  11 us (15%)
  Pallas kernels  3.58 us (5%)
  local copies, waits for them, and re-layouts  2.16 us (3%)
  other arithmetic  1.85 us (2%)
    all_to_all x1, blocking collectives, exchanged(): return lax.all_to_all(pieces, axis, split_axis=0, concat_axis=0, tiled=True)  38.6 us
    ppermute x1, starting transfers between devices, shards(): other = by_rows(lax.ppermute(samples, 'core', swap))  8.74 us
    all_to_all x2, starting transfers between devices, exchanged(): return lax.all_to_all(pieces, axis, split_axis=0, concat_axis=0, tiled=True)  7.04 us
    all_to_all x2, waiting for transfers between devices, exchanged(): return lax.all_to_all(pieces, axis, split_axis=0, concat_axis=0, tiled=True)  6.25 us
    ppermute x1, waiting for transfers between devices, shards(): lax.ppermute(jnp.where(first, samples[:EDGE], other[:EDGE]), TM, ahead_ro...  4.71 us
    pallas_call x3, Pallas kernels, call(): pl.pallas_call(kernel, out_shape=[pltpu.VMEM(shape, dtype) for shape, dty...  3.58 us
  transfers between devices with their start and end apart: 4, of which 2 were waited for; matrix products, arithmetic and copies ran while one was open for 1% of the time, Pallas kernels for 3%

profile of v2, /device:TPU:1, one launch (start us, length us, event | category | flops | bytes accessed | tf_op | source)
XLA Modules:
  0.0 74.3 jit_solution(16777398216695877922)
XLA Ops:
  0.0 8.7 %collective-permute-start = (bf16[512,512]{1,0:T(8,128)(2,1)}, bf16[512,512]{1,0:T(8,128)(2,1)S(1)}, u32[]{:S(2)}, u32[]{:S(2)}) collective-permute-start(bf16[512,512]{1,0:T(8,128)(2,1)} %samples_hbm.1), channel_id=1, source_target_pairs={{0,8},{8,0},{1,9},{9,1},{2,10},{10,2},{3,11},{11,3},{4,12},{12,4},... | collective-permute-start | bytes 1572872 | tf_op jit(solution)/shard_map/ppermute | solution.py:152
  8.7 2.0 %shard_map.28 = (f32[520,128]{1,0:T(8,128)S(1)}, bf16[512,512]{1,0:T(8,128)(2,1)S(1)}) custom-call(bf16[512,512]{1,0:T(8,128)(2,1)} %samples_hbm.1, bf16[4,512,256]{2,1,0:T(8,128)(2,1)} %sketch_hbm.1), custom_call_target="tpu_custom_call" | custom-call | tf_op jit(solution)/shard_map/pallas_call | solution.py:27
  10.8 0.0 collective-permute-done.other_ref
  10.8 0.4 shard_map.29
  11.2 0.0 copy-start
  11.2 1.0 %fusion.2 = f16[1088,128]{1,0:T(8,128)(2,1)} fusion(f32[1088,128]{1,0:T(8,128)S(1)} %shard_map.29), kind=kLoop, calls=%fused_computation.7 | loop fusion | flops 835584 | bytes 835584 | tf_op jit(solution)/shard_map/convert_element_type | solution.py:48
  12.2 3.4 %all-to-all-start = ((f16[8,136,128]{2,1,0:T(8,128)(2,1)}), f16[8,136,128]{2,1,0:T(8,128)(2,1)S(1)}, u32[]{:S(2)}, u32[]{:S(2)}) async-start(f16[8,136,128]{2,1,0:T(8,128)(2,1)} %bitcast), calls=%async_computation | async-start | bytes 557056 | tf_op jit(solution)/shard_map/all_to_all | solution.py:43
  15.6 0.2 copy.7
  15.8 0.2 copy.8
  16.1 6.2 %all-to-all-done = f16[8,136,128]{2,1,0:T(8,128)(2,1)S(1)} async-done(((f16[8,136,128]{2,1,0:T(8,128)(2,1)}), f16[8,136,128]{2,1,0:T(8,128)(2,1)S(1)}, u32[]{:S(2)}, u32[]{:S(2)}) %all-to-all-start) | async-done | bytes 278560 | tf_op jit(solution)/shard_map/all_to_all | solution.py:43
  22.3 0.1 fusion.3
  22.4 0.7 broadcast_in_dim.4
  23.1 3.6 %all-to-all-start.1 = ((bf16[8,136,128]{2,1,0:T(8,128)(2,1)}), bf16[8,136,128]{2,1,0:T(8,128)(2,1)S(1)}, u32[]{:S(2)}, u32[]{:S(2)}) async-start(bf16[8,136,128]{2,1,0:T(8,128)(2,1)} %broadcast_in_dim.4), calls=%async_computation.1 | async-start | bytes 557056 | tf_op jit(solution)/shard_map/all_to_all | solution.py:43
  26.8 0.2 copy.9
  27.0 0.2 copy.10
  27.2 1.3 %collective-permute-start.1 = (bf16[8,512]{0,1:T(8,128)(2,1)S(1)}, bf16[8,512]{0,1:T(8,128)(2,1)S(1)}, u32[]{:S(2)}, u32[]{:S(2)}) collective-permute-start(bf16[8,512]{0,1:T(8,128)(2,1)S(1)} %broadcast_select_fusion), channel_id=1, source_target_pairs={{16,0},{24,8},{32,16},{40,24},{48,32},{56,40},{64,48},{72,56},{80,... | collective-permute-start | bytes 24584 | tf_op jit(solution)/shard_map/ppermute | solution.py:164
  28.5 4.7 %collective-permute-done.1 = bf16[8,512]{0,1:T(8,128)(2,1)S(1)} collective-permute-done((bf16[8,512]{0,1:T(8,128)(2,1)S(1)}, bf16[8,512]{0,1:T(8,128)(2,1)S(1)}, u32[]{:S(2)}, u32[]{:S(2)}) %collective-permute-start.1) | collective-permute-done | bytes 8224 | tf_op jit(solution)/shard_map/ppermute | solution.py:164
  33.2 0.1 bitcast_convert_fusion.sums_ref
  33.3 1.1 %shard_map.30 = f32[512,512]{1,0:T(8,128)S(1)} custom-call(bf16[512,512]{1,0:T(8,128)(2,1)S(1)} %bitcast.17, bf16[512,512]{1,0:T(8,128)(2,1)S(1)} %bitcast.18, bf16[512,128]{1,0:T(8,128)(2,1)S(1)} %pad_bitcast_fusion.tail_ref, f32[1088,128]{1,0:T(8,128)S(1)} %bitcast_convert_fusion.sums_ref), custom_call_target="tpu_custom_call" | custom-call | tf_op jit(solution)/shard_map/pallas_call | solution.py:27
  34.4 0.5 fusion.4
  34.9 38.6 %all_to_all.15 = f16[64,8,512]{2,1,0:T(8,128)(2,1)S(1)} all-to-all(f16[64,8,512]{2,1,0:T(8,128)(2,1)S(1)} %fusion.4), channel_id=1, replica_groups=mesh['y_hi'=4,'z'=8,'core'=2,'y_lo'=2,'x'=4] {'y_hi','z','core'}, dimensions={0} | all-to-all | bytes 1048576 | tf_op jit(solution)/shard_map/all_to_all | solution.py:43
  73.4 0.1 convert_multiply_fusion
  73.6 0.1 fusion.1
  73.7 0.6 copy.11
  (8 shorter events, 0.1 us)
Async XLA Ops:
  0.0 10.8 %collective-permute-start = (bf16[512,512]{1,0:T(8,128)(2,1)}, bf16[512,512]{1,0:T(8,128)(2,1)S(1)}, u32[]{:S(2)}, u32[]{:S(2)}) collective-permute-start(bf16[512,512]{1,0:T(8,128)(2,1)} %samples_hbm.1), channel_id=1, source_target_pairs={{0,8},{8,0},{1,9},{9,1},{2,10},{10,2},{3,11},{11,3},{4,12},{12,4},... | collective-permute-start | bytes 1572872 | tf_op jit(solution)/shard_map/ppermute | solution.py:152
  11.2 4.4 %copy-start = (bf16[512,512]{1,0:T(8,128)(2,1)S(1)}, bf16[512,512]{1,0:T(8,128)(2,1)}, u32[]{:S(2)}) copy-start(bf16[512,512]{1,0:T(8,128)(2,1)} %samples_hbm.1) | copy-start | bytes 1572868
  12.2 10.1 %all-to-all-start = ((f16[8,136,128]{2,1,0:T(8,128)(2,1)}), f16[8,136,128]{2,1,0:T(8,128)(2,1)S(1)}, u32[]{:S(2)}, u32[]{:S(2)}) async-start(f16[8,136,128]{2,1,0:T(8,128)(2,1)} %bitcast), calls=%async_computation | async-start | bytes 557056 | tf_op jit(solution)/shard_map/all_to_all | solution.py:43
  23.1 10.1 %all-to-all-start.1 = ((bf16[8,136,128]{2,1,0:T(8,128)(2,1)}), bf16[8,136,128]{2,1,0:T(8,128)(2,1)S(1)}, u32[]{:S(2)}, u32[]{:S(2)}) async-start(bf16[8,136,128]{2,1,0:T(8,128)(2,1)} %broadcast_in_dim.4), calls=%async_computation.1 | async-start | bytes 557056 | tf_op jit(solution)/shard_map/all_to_all | solution.py:43
  27.2 6.0 %collective-permute-start.1 = (bf16[8,512]{0,1:T(8,128)(2,1)S(1)}, bf16[8,512]{0,1:T(8,128)(2,1)S(1)}, u32[]{:S(2)}, u32[]{:S(2)}) collective-permute-start(bf16[8,512]{0,1:T(8,128)(2,1)S(1)} %broadcast_select_fusion), channel_id=1, source_target_pairs={{16,0},{24,8},{32,16},{40,24},{48,32},{56,40},{64,48},{72,56},{80,... | collective-permute-start | bytes 24584 | tf_op jit(solution)/shard_map/ppermute | solution.py:164

commit v3 on v2

v3 whole, which is shorter than its diff:
```python
import functools

import jax
import jax.numpy as jnp
from jax import lax
from jax.experimental import pallas as pl
from jax.experimental.layout import Layout, with_layout_constraint
from jax.experimental.pallas import tpu as pltpu
from jax.sharding import Mesh
from jax.sharding import PartitionSpec as P


TM = ("y_hi", "z", "core")
CHAN = ("y_lo", "x")
EDGE = 8
LANES = 128
SKETCH_ROOT = 512.0
IMAGE_ROOT = 128.0
ANY = pl.BlockSpec(memory_space=pl.ANY)
VMEM = pl.BlockSpec(memory_space=pltpu.VMEM)


def local_kernel(kernel, out_shapes, scratch, in_vmem=True):
    def call(*args):
        if in_vmem:
            args = [pltpu.with_memory_space_constraint(a, pltpu.VMEM) for a in args]
        return pl.pallas_call(
            kernel,
            out_shape=[pltpu.VMEM(shape, dtype) for shape, dtype in out_shapes],
            in_specs=[VMEM if in_vmem else ANY] * len(args),
            out_specs=[VMEM] * len(out_shapes),
            scratch_shapes=scratch,
        )(*args)

    return call


def by_rows(array):
    return with_layout_constraint(array, Layout(tuple(range(array.ndim))))


def exchanged(pieces, axis):
    return lax.all_to_all(pieces, axis, split_axis=0, concat_axis=0, tiled=True)


def coded(values, root_scale):
    root = jnp.sqrt(jnp.abs(values)) * root_scale
    return jnp.where(values < 0, -root, root).astype(jnp.float16)


def decoded(codes, root_scale):
    root = codes.astype(jnp.float32) * (1.0 / root_scale)
    return root * jnp.abs(root)


def sketched(samples_hbm, sketch_hbm, out_ref, samples_ref, sketch_ref, held, arrivals):
    blocks = sketch_ref.shape[0]
    rows = samples_ref.shape[0]
    halves, reach, width = out_ref.shape
    own = pltpu.make_async_copy(samples_hbm, samples_ref, arrivals.at[blocks])
    loads = [
        pltpu.make_async_copy(sketch_hbm.at[j], sketch_ref.at[j], arrivals.at[j])
        for j in range(blocks)
    ]
    own.start()
    for load in loads:
        load.start()
    for j in range(blocks):
        held[j, :EDGE] = jnp.zeros((EDGE, held.shape[2]), jnp.float32)
        held[j, EDGE + rows :] = jnp.zeros((held.shape[1] - EDGE - rows, held.shape[2]), jnp.float32)
    own.wait()
    for j in range(blocks):
        loads[j].wait()
        held[j, EDGE : EDGE + rows] = jnp.dot(
            samples_ref[...], sketch_ref[j], preferred_element_type=jnp.float32
        )
    for h in range(halves):
        columns = slice(h * width, (h + 1) * width)
        total = held[blocks - 1, EDGE : EDGE + reach, columns]
        for j in range(blocks - 1):
            start = EDGE - (blocks - 1 - j)
            total = total + held[j, start : start + reach, columns]
        out_ref[h] = total


def correlated(block_rows, scale, own_ref, other_ref, tail_ref, sums_ref, out_ref, held, steps):
    parts, cores, part, width = sums_ref.shape
    rows = own_ref.shape[1]
    core = lax.axis_index("core")
    mine = pl.ds(pl.multiple_of(core * rows, rows), rows)
    theirs = pl.ds(pl.multiple_of((cores - 1 - core) * rows, rows), rows)
    ends = pl.ds(cores * rows, tail_ref.shape[1])
    depth = cores * rows + 2 * EDGE
    held[:EDGE] = jnp.zeros((EDGE, width), jnp.float32)
    held[EDGE + parts * part :] = jnp.zeros((held.shape[0] - EDGE - parts * part, width), jnp.float32)
    for k in range(cores):
        for n in range(parts):
            start = EDGE + k * rows + n * part
            there = slice(start, start + part)
            held[there] = sums_ref[n, k] if k == 0 else held[there] + sums_ref[n, k]
    steps[depth:] = jnp.zeros((steps.shape[0] - depth, steps.shape[1]), steps.dtype)
    for i in range(block_rows):
        moved = held[EDGE - 1 - i : EDGE - 1 - i + depth]
        steps[:depth, i * width : (i + 1) * width] = moved.astype(steps.dtype)
    wide = 2 * width
    for i in range(0, block_rows * width, wide):
        found = jnp.zeros((out_ref.shape[0], wide), jnp.float32)
        for turned, where in ((own_ref, mine), (other_ref, theirs), (tail_ref, ends)):
            found = found + jnp.dot(
                turned[...], steps[where, i : i + wide], preferred_element_type=jnp.float32
            )
        out_ref[:, i : i + wide] = found * scale


def shards(samples, sketch):
    rows, local = samples.shape
    blocks, _, width = sketch.shape
    cores = lax.axis_size("core")
    near = lax.axis_size(CHAN)
    groups = lax.axis_size(TM)
    half = width // cores
    part = -(-(rows + blocks - 1) // (near * EDGE)) * EDGE
    reach = near * part
    swap = [(i, cores - 1 - i) for i in range(cores)]
    chips = range(0, groups - cores, cores)

    (partial,) = local_kernel(
        sketched,
        [((cores, reach, half), jnp.float32)],
        [
            pltpu.VMEM(samples.shape, samples.dtype),
            pltpu.VMEM(sketch.shape, sketch.dtype),
            pltpu.VMEM((blocks, reach + 2 * EDGE, width), jnp.float32),
            pltpu.SemaphoreType.DMA((blocks + 1,)),
        ],
        in_vmem=False,
    )(samples, sketch)
    pieces = coded(partial, SKETCH_ROOT).reshape(cores * near, part, half)
    arrived = exchanged(pieces, ("core", *CHAN)).reshape(cores, near, part, half)
    other = by_rows(lax.ppermute(samples, "core", swap))
    heads = []
    for core in range(cores):
        route = [(i + cores, i + core) for i in chips]
        heads.append(lax.ppermute(samples[:EDGE], TM, route))
    ahead = sum(heads[1:], heads[0])
    total = decoded(arrived, SKETCH_ROOT).sum(1).astype(jnp.bfloat16)
    total = total.reshape(cores * part, half)
    total, *turned = lax.optimization_barrier((total, samples.T, other.T))
    tail = jnp.pad(ahead, ((0, LANES - EDGE), (0, 0)))
    sums = exchanged(jnp.broadcast_to(total[None], (near, cores * part, half)), CHAN)
    sums = sums.astype(jnp.float32).reshape(near, cores, part, half)
    scale = 1.0 / (rows * groups) ** 0.5
    (found,) = local_kernel(
        functools.partial(correlated, blocks, scale),
        [((local, blocks * half), jnp.float32)],
        [
            pltpu.VMEM((EDGE + (cores - 1) * rows + reach, half), jnp.float32),
            pltpu.VMEM((cores * rows + LANES, blocks * half), jnp.bfloat16),
        ],
    )(*turned, tail.T, sums)
    pieces = coded(found, IMAGE_ROOT).reshape(groups, local // groups, blocks * half)
    landed = exchanged(pieces, TM)
    landed = landed.reshape(groups // cores, cores, local // groups, blocks, half)
    mine = decoded(landed, IMAGE_ROOT).sum(0)
    return jnp.concatenate([mine[k] for k in range(cores)], -1)[None]


def solution(mesh):
    sizes = {"y_hi": 4, "z": 8, "core": 2, "y_lo": 2, "x": 4}
    fine = Mesh(mesh.devices.reshape(tuple(sizes.values())), tuple(sizes))
    placed = (P(TM, CHAN), P(None, CHAN, None))
    return jax.shard_map(shards, mesh=fine, in_specs=placed, out_specs=P(CHAN, TM, None, None), check_vma=False)
```

time: 74.7 us -> 74.6 us (level)
  waiting for transfers between devices: 11 us -> 10.2 us
    ppermute x1, starting transfers between devices: 8.74 us -> 2.08 us  [shards(): other = by_rows(lax.ppermute(samples, 'core', swap))]
    all_to_all x2, starting transfers between devices: 7.04 us -> 13.6 us  [exchanged(): return lax.all_to_all(pieces, axis, split_axis=0, concat_axis=0, tiled=True)]
    all_to_all x2, waiting for transfers between devices: 6.25 us -> 4.12 us  [exchanged(): return lax.all_to_all(pieces, axis, split_axis=0, concat_axis=0, tiled=True)]
    ppermute x1, waiting for transfers between devices: 0.01 us -> 1.49 us  [shards(): other = by_rows(lax.ppermute(samples, 'core', swap))]
    ppermute x1 -> x2, starting transfers between devices: 1.29 us -> 1.96 us  [shards(): heads.append(lax.ppermute(samples[:EDGE], TM, route))]
    pallas_call x3 -> x2, Pallas kernels: 3.58 us -> 3.97 us  [call(): pl.pallas_call(kernel, out_shape=[pltpu.VMEM(shape, dtype) for shape, dty...]
    ppermute x1 -> x2, waiting for transfers between devices: 4.71 us -> 4.61 us  [shards(): heads.append(lax.ppermute(samples[:EDGE], TM, route))]
  transfers between devices with their start and end apart: 4 -> 5, of which waited for: 2 -> 3; matrix products, arithmetic and copies ran while one was open for 1% -> 1% of each run, Pallas kernels for 3% -> 0%
where the time goes in v3:
time: 74.6 us; the launch traced here: 74.2 us
  blocking collectives  38.5 us (52%)
  starting transfers between devices  17.7 us (24%)
  waiting for transfers between devices  10.2 us (14%)
  Pallas kernels  3.97 us (5%)
  other arithmetic  1.88 us (3%)
  local copies, waits for them, and re-layouts  1.86 us (2%)
    all_to_all x1, blocking collectives, exchanged(): return lax.all_to_all(pieces, axis, split_axis=0, concat_axis=0, tiled=True)  38.5 us
    all_to_all x2, starting transfers between devices, exchanged(): return lax.all_to_all(pieces, axis, split_axis=0, concat_axis=0, tiled=True)  13.6 us
    ppermute x2, waiting for transfers between devices, shards(): heads.append(lax.ppermute(samples[:EDGE], TM, route))  4.61 us
    all_to_all x2, waiting for transfers between devices, exchanged(): return lax.all_to_all(pieces, axis, split_axis=0, concat_axis=0, tiled=True)  4.12 us
    pallas_call x2, Pallas kernels, call(): pl.pallas_call(kernel, out_shape=[pltpu.VMEM(shape, dtype) for shape, dty...  3.97 us
    ppermute x1, starting transfers between devices, shards(): other = by_rows(lax.ppermute(samples, 'core', swap))  2.08 us
    ppermute x2, starting transfers between devices, shards(): heads.append(lax.ppermute(samples[:EDGE], TM, route))  1.96 us
    ppermute x1, waiting for transfers between devices, shards(): other = by_rows(lax.ppermute(samples, 'core', swap))  1.49 us
  transfers between devices with their start and end apart: 5, of which 3 were waited for; matrix products, arithmetic and copies ran while one was open for 1% of the time, Pallas kernels for 0%

profile of v3, /device:TPU:1, one launch (start us, length us, event | category | flops | bytes accessed | tf_op | source)
XLA Modules:
  0.0 74.2 jit_solution(12975988662749135500)
XLA Ops:
  0.0 2.8 %shard_map.28 = f32[2,576,128]{2,1,0:T(8,128)S(1)} custom-call(bf16[512,512]{1,0:T(8,128)(2,1)} %samples_hbm.1, bf16[4,512,256]{2,1,0:T(8,128)(2,1)} %sketch_hbm.1), custom_call_target="tpu_custom_call" | custom-call | tf_op jit(solution)/shard_map/pallas_call | solution.py:27
  2.9 0.0 copy-start
  2.9 1.0 %fusion.2 = f16[2,576,128]{2,1,0:T(8,128)(2,1)} fusion(f32[2,576,128]{2,1,0:T(8,128)S(1)} %shard_map.28), kind=kLoop, calls=%fused_computation.7 | loop fusion | flops 884736 | bytes 884736 | tf_op jit(solution)/shard_map/convert_element_type | solution.py:48
  3.9 10.2 %all-to-all-start = ((f16[16,72,128]{2,1,0:T(8,128)(2,1)}), f16[16,72,128]{2,1,0:T(8,128)(2,1)S(1)}, u32[]{:S(2)}, u32[]{:S(2)}) async-start(f16[16,72,128]{2,1,0:T(8,128)(2,1)} %bitcast), calls=%async_computation | async-start | bytes 589824 | tf_op jit(solution)/shard_map/all_to_all | solution.py:43
  14.1 0.0 copy-done
  14.1 2.1 %collective-permute-start = (bf16[512,512]{1,0:T(8,128)(2,1)S(1)}, bf16[512,512]{1,0:T(8,128)(2,1)S(1)}, u32[]{:S(2)}, u32[]{:S(2)}) collective-permute-start(bf16[512,512]{1,0:T(8,128)(2,1)S(1)} %copy-done), channel_id=1, source_target_pairs={{0,8},{8,0},{1,9},{9,1},{2,10},{10,2},{3,11},{11,3},{4,12},{12,4},... | collective-permute-start | bytes 1572872 | tf_op jit(solution)/shard_map/ppermute | solution.py:140
  16.2 0.2 copy.6
  16.4 1.5 %collective-permute-done = bf16[512,512]{1,0:T(8,128)(2,1)S(1)} collective-permute-done((bf16[512,512]{1,0:T(8,128)(2,1)S(1)}, bf16[512,512]{1,0:T(8,128)(2,1)S(1)}, u32[]{:S(2)}, u32[]{:S(2)}) %collective-permute-start) | collective-permute-done | bytes 524320 | tf_op jit(solution)/shard_map/ppermute | solution.py:140
  17.9 0.2 copy.7
  18.1 4.1 %all-to-all-done = f16[16,72,128]{2,1,0:T(8,128)(2,1)S(1)} async-done(((f16[16,72,128]{2,1,0:T(8,128)(2,1)}), f16[16,72,128]{2,1,0:T(8,128)(2,1)S(1)}, u32[]{:S(2)}, u32[]{:S(2)}) %all-to-all-start) | async-done | bytes 294944 | tf_op jit(solution)/shard_map/all_to_all | solution.py:43
  22.2 0.1 fusion.3
  22.3 0.7 %broadcast_in_dim.4 = bf16[8,144,128]{2,1,0:T(8,128)(2,1)} broadcast(bf16[144,128]{1,0:T(8,128)(2,1)S(1)} %bitcast.23), dimensions={1,2} | broadcast | bytes 331776 | tf_op jit(solution)/shard_map/broadcast_in_dim | solution.py:150
  23.0 3.4 %all-to-all-start.1 = ((bf16[8,144,128]{2,1,0:T(8,128)(2,1)}), bf16[8,144,128]{2,1,0:T(8,128)(2,1)S(1)}, u32[]{:S(2)}, u32[]{:S(2)}) async-start(bf16[8,144,128]{2,1,0:T(8,128)(2,1)} %broadcast_in_dim.4), calls=%async_computation.1 | async-start | bytes 589824 | tf_op jit(solution)/shard_map/all_to_all | solution.py:43
  26.5 1.3 %collective-permute-start.2 = (bf16[8,512]{0,1:T(8,128)(2,1)S(1)}, bf16[8,512]{0,1:T(8,128)(2,1)S(1)}, u32[]{:S(2)}, u32[]{:S(2)}) collective-permute-start(bf16[8,512]{0,1:T(8,128)(2,1)S(1)} %slice.13), channel_id=1, source_target_pairs={{16,8},{32,24},{48,40},{64,56},{80,72},{96,88},{112,104},{128,120}... | collective-permute-start | bytes 24584 | tf_op jit(solution)/shard_map/ppermute | solution.py:144
  27.8 0.7 collective-permute-start.1
  28.5 4.6 %collective-permute-done.2 = bf16[8,512]{0,1:T(8,128)(2,1)S(1)} collective-permute-done((bf16[8,512]{0,1:T(8,128)(2,1)S(1)}, bf16[8,512]{0,1:T(8,128)(2,1)S(1)}, u32[]{:S(2)}, u32[]{:S(2)}) %collective-permute-start.2) | collective-permute-done | bytes 8224 | tf_op jit(solution)/shard_map/ppermute | solution.py:144
  33.1 0.0 collective-permute-done.1
  33.1 0.0 all-to-all-done.1
  33.2 1.1 %shard_map.29 = f32[512,512]{1,0:T(8,128)S(1)} custom-call(bf16[512,512]{1,0:T(8,128)(2,1)S(1)} %bitcast.19, bf16[512,512]{1,0:T(8,128)(2,1)S(1)} %bitcast.20, bf16[512,128]{1,0:T(8,128)(2,1)S(1)} %pad_bitcast_fusion.tail_ref, f32[8,2,72,128]{3,2,1,0:T(8,128)S(1)} %convert.1.sums_ref), custom_call_target="tpu_custom_call" | custom-call | tf_op jit(solution)/shard_map/pallas_call | solution.py:27
  34.4 0.5 fusion.4
  34.8 38.5 %all_to_all.15 = f16[64,8,512]{2,1,0:T(8,128)(2,1)S(1)} all-to-all(f16[64,8,512]{2,1,0:T(8,128)(2,1)S(1)} %fusion.4), channel_id=1, replica_groups=mesh['y_hi'=4,'z'=8,'core'=2,'y_lo'=2,'x'=4] {'y_hi','z','core'}, dimensions={0} | all-to-all | bytes 1048576 | tf_op jit(solution)/shard_map/all_to_all | solution.py:43
  73.3 0.1 convert_multiply_fusion
  73.4 0.1 fusion.1
  73.6 0.6 copy.9
  (6 shorter events, 0.1 us)
Async XLA Ops:
  2.9 11.2 %copy-start = (bf16[512,512]{1,0:T(8,128)(2,1)S(1)}, bf16[512,512]{1,0:T(8,128)(2,1)}, u32[]{:S(2)}) copy-start(bf16[512,512]{1,0:T(8,128)(2,1)} %samples_hbm.1) | copy-start | bytes 1572868
  3.9 18.3 %all-to-all-start = ((f16[16,72,128]{2,1,0:T(8,128)(2,1)}), f16[16,72,128]{2,1,0:T(8,128)(2,1)S(1)}, u32[]{:S(2)}, u32[]{:S(2)}) async-start(f16[16,72,128]{2,1,0:T(8,128)(2,1)} %bitcast), calls=%async_computation | async-start | bytes 589824 | tf_op jit(solution)/shard_map/all_to_all | solution.py:43
  14.1 3.8 %collective-permute-start = (bf16[512,512]{1,0:T(8,128)(2,1)S(1)}, bf16[512,512]{1,0:T(8,128)(2,1)S(1)}, u32[]{:S(2)}, u32[]{:S(2)}) collective-permute-start(bf16[512,512]{1,0:T(8,128)(2,1)S(1)} %copy-done), channel_id=1, source_target_pairs={{0,8},{8,0},{1,9},{9,1},{2,10},{10,2},{3,11},{11,3},{4,12},{12,4},... | collective-permute-start | bytes 1572872 | tf_op jit(solution)/shard_map/ppermute | solution.py:140
  23.0 10.2 %all-to-all-start.1 = ((bf16[8,144,128]{2,1,0:T(8,128)(2,1)}), bf16[8,144,128]{2,1,0:T(8,128)(2,1)S(1)}, u32[]{:S(2)}, u32[]{:S(2)}) async-start(bf16[8,144,128]{2,1,0:T(8,128)(2,1)} %broadcast_in_dim.4), calls=%async_computation.1 | async-start | bytes 589824 | tf_op jit(solution)/shard_map/all_to_all | solution.py:43
  26.5 6.6 %collective-permute-start.2 = (bf16[8,512]{0,1:T(8,128)(2,1)S(1)}, bf16[8,512]{0,1:T(8,128)(2,1)S(1)}, u32[]{:S(2)}, u32[]{:S(2)}) collective-permute-start(bf16[8,512]{0,1:T(8,128)(2,1)S(1)} %slice.13), channel_id=1, source_target_pairs={{16,8},{32,24},{48,40},{64,56},{80,72},{96,88},{112,104},{128,120}... | collective-permute-start | bytes 24584 | tf_op jit(solution)/shard_map/ppermute | solution.py:144
  27.8 5.3 %collective-permute-start.1 = (bf16[8,512]{0,1:T(8,128)(2,1)S(1)}, bf16[8,512]{0,1:T(8,128)(2,1)S(1)}, u32[]{:S(2)}, u32[]{:S(2)}) collective-permute-start(bf16[8,512]{0,1:T(8,128)(2,1)S(1)} %slice.13), channel_id=1, source_target_pairs={{16,0},{32,16},{48,32},{64,48},{80,64},{96,80},{112,96},{128,112},... | collective-permute-start | bytes 24584 | tf_op jit(solution)/shard_map/ppermute | solution.py:144

commit v4 on v2

--- a/solution.py
+++ b/solution.py
@@ -53,11 +53,11 @@
     return root * jnp.abs(root)
 
 
-def shifted_sum(held, reach, width):
+def shifted_sum(held, first, reach, width):
     blocks = held.shape[1] // width
-    total = held[EDGE : EDGE + reach, (blocks - 1) * width :]
+    total = held[EDGE + first : EDGE + first + reach, (blocks - 1) * width :]
     for j in range(blocks - 1):
-        start = EDGE - (blocks - 1 - j)
+        start = EDGE + first - (blocks - 1 - j)
         total = total + held[start : start + reach, j * width : (j + 1) * width]
     return total
 
@@ -72,7 +72,13 @@
     rows = samples_ref.shape[0]
     reach, width = own_ref.shape
     start = pl.multiple_of(lax.axis_index("core") * width, width)
-    rows_load = pltpu.make_async_copy(samples_hbm, samples_ref, arrivals.at[blocks])
+    step = rows // 2
+    rows_loads = [
+        pltpu.make_async_copy(
+            samples_hbm.at[n : n + step], samples_ref.at[n : n + step], arrivals.at[blocks + n // step]
+        )
+        for n in range(0, rows, step)
+    ]
     loads = [
         pltpu.make_async_copy(
             sketch_hbm.at[j, :, pl.ds(start, width)],
@@ -81,19 +87,19 @@
         )
         for j in range(blocks)
     ]
-    rows_load.start()
-    for load in loads:
+    rows_loads[0].start()
+    for load in loads + rows_loads[1:]:
         load.start()
     clear_edges(held, rows)
-    rows_load.wait()
-    for j in range(0, blocks, 2):
-        pair = slice(j * width, (j + 2) * width)
-        for load in loads[j : j + 2]:
-            load.wait()
-        held[EDGE : EDGE + rows, pair] = jnp.dot(
-            samples_ref[...], columns_ref[:, pair], preferred_element_type=jnp.float32
+    for load in loads:
+        load.wait()
+    for n, load in zip(range(0, rows, step), rows_loads):
+        load.wait()
+        held[EDGE + n : EDGE + n + step] = jnp.dot(
+            samples_ref[n : n + step], columns_ref[...], preferred_element_type=jnp.float32
         )
-    own_ref[...] = shifted_sum(held, reach, width)
+        end = n + step if n + step < rows else reach
+        own_ref[n:end] = shifted_sum(held, n, end - n, width)
 
 
 def sketched_chip(other_ref, columns_ref, own_ref, out_ref, held):
@@ -109,7 +115,7 @@
     theirs = pl.ds(pl.multiple_of((cores - 1 - core) * rows, rows), reach)
     out_ref[...] = jnp.zeros_like(out_ref)
     out_ref[mine] = own_ref[...]
-    out_ref[theirs] = out_ref[theirs] + shifted_sum(held, reach, width)
+    out_ref[theirs] = out_ref[theirs] + shifted_sum(held, 0, reach, width)
 
 
 def correlated(block_rows, scale, own_ref, other_ref, tail_ref, sums_ref, out_ref, held, steps):
@@ -154,12 +160,10 @@
     own, columns = local_kernel(
         sketched_own,
         [((rows + EDGE, half), jnp.float32), ((local, blocks * half), sketch.dtype)],
-        [pltpu.VMEM(samples.shape, samples.dtype), held, pltpu.SemaphoreType.DMA((blocks + 1,))],
+        [pltpu.VMEM(samples.shape, samples.dtype), held, pltpu.SemaphoreType.DMA((blocks + 2,))],
         in_vmem=False,
     )(samples, sketch)
-    (partial,) = local_kernel(
-        sketched_chip, [((reach, half), jnp.float32)], [held]
-    )(other, columns, own)
+    (partial,) = local_kernel(sketched_chip, [((reach, half), jnp.float32)], [held])(other, columns, own)
     first = lax.axis_index("core") == 0
     ahead = lax.ppermute(jnp.where(first, samples[:EDGE], other[:EDGE]), TM, ahead_route)
     arrived = exchanged(coded(partial, SKETCH_ROOT).reshape(near, part, half), CHAN)
@@ -179,8 +183,8 @@
     )(*turned, tail.T, sums)
     pieces = coded(found, IMAGE_ROOT).reshape(groups, local // groups, blocks * half)
     landed = exchanged(pieces, TM)
-    landed = landed.reshape(groups // cores, cores, local // groups, blocks, half)
-    mine = decoded(landed, IMAGE_ROOT).sum(0)
+    landed = landed.reshape(groups // cores, cores, local // groups, blocks * half)
+    mine = decoded(landed, IMAGE_ROOT).sum(0).reshape(cores, local // groups, blocks, half)
     return jnp.concatenate([mine[k] for k in range(cores)], -1)[None]
 
 
@@ -188,6 +192,4 @@
     sizes = {"y_hi": 4, "z": 8, "core": 2, "y_lo": 2, "x": 4}
     fine = Mesh(mesh.devices.reshape(tuple(sizes.values())), tuple(sizes))
     placed = (P(TM, CHAN), P(None, CHAN, None))
-    return jax.shard_map(
-        shards, mesh=fine, in_specs=placed, out_specs=P(CHAN, TM, None, None), check_vma=False
-    )
+    return jax.shard_map(shards, mesh=fine, in_specs=placed, out_specs=P(CHAN, TM, None, None), check_vma=False)

time: 74.7 us -> 74.5 us (level)
  transfers between devices with their start and end apart: 4 -> 4, of which waited for: 2 -> 2; matrix products, arithmetic and copies ran while one was open for 1% -> 1% of each run, Pallas kernels for 3% -> 2%
where the time goes in v4:
time: 74.5 us; the launch traced here: 74.1 us
  blocking collectives  38.5 us (52%)
  starting transfers between devices  17.6 us (24%)
  waiting for transfers between devices  10.5 us (14%)
  Pallas kernels  3.39 us (5%)
  other arithmetic  2.47 us (3%)
  local copies, waits for them, and re-layouts  1.55 us (2%)
    all_to_all x1, blocking collectives, exchanged(): return lax.all_to_all(pieces, axis, split_axis=0, concat_axis=0, tiled=True)  38.5 us
    ppermute x1, starting transfers between devices, shards(): other = by_rows(lax.ppermute(samples, 'core', swap))  8.74 us
    all_to_all x2, starting transfers between devices, exchanged(): return lax.all_to_all(pieces, axis, split_axis=0, concat_axis=0, tiled=True)  7.52 us
    all_to_all x2, waiting for transfers between devices, exchanged(): return lax.all_to_all(pieces, axis, split_axis=0, concat_axis=0, tiled=True)  5.75 us
    ppermute x1, waiting for transfers between devices, shards(): lax.ppermute(jnp.where(first, samples[:EDGE], other[:EDGE]), TM, ahead_ro...  4.71 us
    pallas_call x3, Pallas kernels, call(): pl.pallas_call(kernel, out_shape=[pltpu.VMEM(shape, dtype) for shape, dty...  3.39 us
  transfers between devices with their start and end apart: 4, of which 2 were waited for; matrix products, arithmetic and copies ran while one was open for 1% of the time, Pallas kernels for 2%

profile of v4, /device:TPU:1, one launch (start us, length us, event | category | flops | bytes accessed | tf_op | source)
XLA Modules:
  0.0 74.1 jit_solution(3929291446253958382)
XLA Ops:
  0.0 8.7 %collective-permute-start = (bf16[512,512]{1,0:T(8,128)(2,1)}, bf16[512,512]{1,0:T(8,128)(2,1)S(1)}, u32[]{:S(2)}, u32[]{:S(2)}) collective-permute-start(bf16[512,512]{1,0:T(8,128)(2,1)} %samples_hbm.1), channel_id=1, source_target_pairs={{0,8},{8,0},{1,9},{9,1},{2,10},{10,2},{3,11},{11,3},{4,12},{12,4},... | collective-permute-start | bytes 1572872 | tf_op jit(solution)/shard_map/ppermute | solution.py:158
  8.7 1.8 %shard_map.28 = (f32[520,128]{1,0:T(8,128)S(1)}, bf16[512,512]{1,0:T(8,128)(2,1)S(1)}) custom-call(bf16[512,512]{1,0:T(8,128)(2,1)} %samples_hbm.1, bf16[4,512,256]{2,1,0:T(8,128)(2,1)} %sketch_hbm.1), custom_call_target="tpu_custom_call" | custom-call | tf_op jit(solution)/shard_map/pallas_call | solution.py:27
  10.6 0.0 collective-permute-done.other_ref
  10.6 0.4 shard_map.29
  11.0 0.0 copy-start
  11.1 1.0 %fusion.2 = f16[1088,128]{1,0:T(8,128)(2,1)} fusion(f32[1088,128]{1,0:T(8,128)S(1)} %shard_map.29), kind=kLoop, calls=%fused_computation.7 | loop fusion | flops 835584 | bytes 835584 | tf_op jit(solution)/shard_map/convert_element_type | solution.py:48
  12.0 3.4 %all-to-all-start = ((f16[8,136,128]{2,1,0:T(8,128)(2,1)}), f16[8,136,128]{2,1,0:T(8,128)(2,1)S(1)}, u32[]{:S(2)}, u32[]{:S(2)}) async-start(f16[8,136,128]{2,1,0:T(8,128)(2,1)} %bitcast), calls=%async_computation | async-start | bytes 557056 | tf_op jit(solution)/shard_map/all_to_all | solution.py:43
  15.5 0.2 copy.3
  15.7 0.2 copy.4
  15.9 5.7 %all-to-all-done = f16[8,136,128]{2,1,0:T(8,128)(2,1)S(1)} async-done(((f16[8,136,128]{2,1,0:T(8,128)(2,1)}), f16[8,136,128]{2,1,0:T(8,128)(2,1)S(1)}, u32[]{:S(2)}, u32[]{:S(2)}) %all-to-all-start) | async-done | bytes 278560 | tf_op jit(solution)/shard_map/all_to_all | solution.py:43
  21.6 0.1 fusion.3
  21.7 0.7 broadcast_in_dim.4
  22.5 4.1 %all-to-all-start.1 = ((bf16[8,136,128]{2,1,0:T(8,128)(2,1)}), bf16[8,136,128]{2,1,0:T(8,128)(2,1)S(1)}, u32[]{:S(2)}, u32[]{:S(2)}) async-start(bf16[8,136,128]{2,1,0:T(8,128)(2,1)} %broadcast_in_dim.4), calls=%async_computation.1 | async-start | bytes 557056 | tf_op jit(solution)/shard_map/all_to_all | solution.py:43
  26.6 0.2 copy.5
  26.8 0.2 copy.6
  27.0 1.3 %collective-permute-start.1 = (bf16[8,512]{0,1:T(8,128)(2,1)S(1)}, bf16[8,512]{0,1:T(8,128)(2,1)S(1)}, u32[]{:S(2)}, u32[]{:S(2)}) collective-permute-start(bf16[8,512]{0,1:T(8,128)(2,1)S(1)} %broadcast_select_fusion), channel_id=1, source_target_pairs={{16,0},{24,8},{32,16},{40,24},{48,32},{56,40},{64,48},{72,56},{80,... | collective-permute-start | bytes 24584 | tf_op jit(solution)/shard_map/ppermute | solution.py:168
  28.3 4.7 %collective-permute-done.1 = bf16[8,512]{0,1:T(8,128)(2,1)S(1)} collective-permute-done((bf16[8,512]{0,1:T(8,128)(2,1)S(1)}, bf16[8,512]{0,1:T(8,128)(2,1)S(1)}, u32[]{:S(2)}, u32[]{:S(2)}) %collective-permute-start.1) | collective-permute-done | bytes 8224 | tf_op jit(solution)/shard_map/ppermute | solution.py:168
  33.0 0.1 bitcast_convert_fusion.sums_ref
  33.1 1.1 %shard_map.30 = f32[512,512]{1,0:T(8,128)S(1)} custom-call(bf16[512,512]{1,0:T(8,128)(2,1)S(1)} %bitcast.13, bf16[512,512]{1,0:T(8,128)(2,1)S(1)} %bitcast.14, bf16[512,128]{1,0:T(8,128)(2,1)S(1)} %pad_bitcast_fusion.tail_ref, f32[1088,128]{1,0:T(8,128)S(1)} %bitcast_convert_fusion.sums_ref), custom_call_target="tpu_custom_call" | custom-call | tf_op jit(solution)/shard_map/pallas_call | solution.py:27
  34.2 0.5 fusion.4
  34.7 38.5 %all_to_all.15 = f16[64,8,512]{2,1,0:T(8,128)(2,1)S(1)} all-to-all(f16[64,8,512]{2,1,0:T(8,128)(2,1)S(1)} %fusion.4), channel_id=1, replica_groups=mesh['y_hi'=4,'z'=8,'core'=2,'y_lo'=2,'x'=4] {'y_hi','z','core'}, dimensions={0} | all-to-all | bytes 1048576 | tf_op jit(solution)/shard_map/all_to_all | solution.py:43
  73.1 0.1 convert_multiply_fusion
  73.3 0.1 fusion.1
  73.4 0.6 maximum_bitcast_fusion
  (9 shorter events, 0.1 us)
Async XLA Ops:
  0.0 10.6 %collective-permute-start = (bf16[512,512]{1,0:T(8,128)(2,1)}, bf16[512,512]{1,0:T(8,128)(2,1)S(1)}, u32[]{:S(2)}, u32[]{:S(2)}) collective-permute-start(bf16[512,512]{1,0:T(8,128)(2,1)} %samples_hbm.1), channel_id=1, source_target_pairs={{0,8},{8,0},{1,9},{9,1},{2,10},{10,2},{3,11},{11,3},{4,12},{12,4},... | collective-permute-start | bytes 1572872 | tf_op jit(solution)/shard_map/ppermute | solution.py:158
  11.0 4.4 %copy-start = (bf16[512,512]{1,0:T(8,128)(2,1)S(1)}, bf16[512,512]{1,0:T(8,128)(2,1)}, u32[]{:S(2)}) copy-start(bf16[512,512]{1,0:T(8,128)(2,1)} %samples_hbm.1) | copy-start | bytes 1572868
  12.0 9.6 %all-to-all-start = ((f16[8,136,128]{2,1,0:T(8,128)(2,1)}), f16[8,136,128]{2,1,0:T(8,128)(2,1)S(1)}, u32[]{:S(2)}, u32[]{:S(2)}) async-start(f16[8,136,128]{2,1,0:T(8,128)(2,1)} %bitcast), calls=%async_computation | async-start | bytes 557056 | tf_op jit(solution)/shard_map/all_to_all | solution.py:43
  22.5 10.5 %all-to-all-start.1 = ((bf16[8,136,128]{2,1,0:T(8,128)(2,1)}), bf16[8,136,128]{2,1,0:T(8,128)(2,1)S(1)}, u32[]{:S(2)}, u32[]{:S(2)}) async-start(bf16[8,136,128]{2,1,0:T(8,128)(2,1)} %broadcast_in_dim.4), calls=%async_computation.1 | async-start | bytes 557056 | tf_op jit(solution)/shard_map/all_to_all | solution.py:43
  27.0 6.0 %collective-permute-start.1 = (bf16[8,512]{0,1:T(8,128)(2,1)S(1)}, bf16[8,512]{0,1:T(8,128)(2,1)S(1)}, u32[]{:S(2)}, u32[]{:S(2)}) collective-permute-start(bf16[8,512]{0,1:T(8,128)(2,1)S(1)} %broadcast_select_fusion), channel_id=1, source_target_pairs={{16,0},{24,8},{32,16},{40,24},{48,32},{56,40},{64,48},{72,56},{80,... | collective-permute-start | bytes 24584 | tf_op jit(solution)/shard_map/ppermute | solution.py:168

commit v5 on v4

--- a/solution.py
+++ b/solution.py
@@ -43,14 +43,15 @@
     return lax.all_to_all(pieces, axis, split_axis=0, concat_axis=0, tiled=True)
 
 
-def coded(values, root_scale):
+def rooted(values, root_scale):
     root = jnp.sqrt(jnp.abs(values)) * root_scale
-    return jnp.where(values < 0, -root, root).astype(jnp.float16)
+    return jnp.where(values < 0, -root, root)
 
 
-def decoded(codes, root_scale):
-    root = codes.astype(jnp.float32) * (1.0 / root_scale)
-    return root * jnp.abs(root)
+def squared(codes, root_scale):
+    root = codes.astype(jnp.float32)
+    square = root * root
+    return jnp.where(root < 0, -square, square) * (1.0 / root_scale**2)
 
 
 def shifted_sum(held, first, reach, width):
@@ -116,6 +117,7 @@
     out_ref[...] = jnp.zeros_like(out_ref)
     out_ref[mine] = own_ref[...]
     out_ref[theirs] = out_ref[theirs] + shifted_sum(held, 0, reach, width)
+    out_ref[...] = rooted(out_ref[...], SKETCH_ROOT)
 
 
 def correlated(block_rows, scale, own_ref, other_ref, tail_ref, sums_ref, out_ref, held, steps):
@@ -140,7 +142,7 @@
             found = found + jnp.dot(
                 turned[...], steps[where, i : i + wide], preferred_element_type=jnp.float32
             )
-        out_ref[:, i : i + wide] = found * scale
+        out_ref[:, i : i + wide] = rooted(found * scale, IMAGE_ROOT)
 
 
 def shards(samples, sketch):
@@ -166,8 +168,8 @@
     (partial,) = local_kernel(sketched_chip, [((reach, half), jnp.float32)], [held])(other, columns, own)
     first = lax.axis_index("core") == 0
     ahead = lax.ppermute(jnp.where(first, samples[:EDGE], other[:EDGE]), TM, ahead_route)
-    arrived = exchanged(coded(partial, SKETCH_ROOT).reshape(near, part, half), CHAN)
-    total = decoded(arrived, SKETCH_ROOT).sum(0).astype(jnp.bfloat16)
+    arrived = exchanged(partial.astype(jnp.float16).reshape(near, part, half), CHAN)
+    total = squared(arrived, SKETCH_ROOT).sum(0).astype(jnp.bfloat16)
     total, *turned = lax.optimization_barrier((total, samples.T, other.T))
     tail = jnp.pad(ahead, ((0, LANES - EDGE), (0, 0)))
     sums = exchanged(jnp.broadcast_to(total[None], (near, part, half)), CHAN)
@@ -181,10 +183,11 @@
             pltpu.VMEM((cores * rows + LANES, blocks * half), jnp.bfloat16),
         ],
     )(*turned, tail.T, sums)
-    pieces = coded(found, IMAGE_ROOT).reshape(groups, local // groups, blocks * half)
+    pieces = found.astype(jnp.float16).reshape(groups, local // groups, blocks * half)
     landed = exchanged(pieces, TM)
     landed = landed.reshape(groups // cores, cores, local // groups, blocks * half)
-    mine = decoded(landed, IMAGE_ROOT).sum(0).reshape(cores, local // groups, blocks, half)
+    landed = lax.optimization_barrier(landed)
+    mine = squared(landed, IMAGE_ROOT).sum(0).reshape(cores, local // groups, blocks, half)
     return jnp.concatenate([mine[k] for k in range(cores)], -1)[None]
 
 

time: 74.5 us -> 74.6 us (level)
  no operation moved by 1% of the time
where the time goes in v5:
time: 74.6 us; the launch traced here: 74.2 us
  blocking collectives  38.5 us (52%)
  starting transfers between devices  17.5 us (23%)
  waiting for transfers between devices  10.5 us (14%)
  Pallas kernels  4.05 us (5%)
  other arithmetic  1.91 us (3%)
  local copies, waits for them, and re-layouts  1.56 us (2%)
    all_to_all x1, blocking collectives, exchanged(): return lax.all_to_all(pieces, axis, split_axis=0, concat_axis=0, tiled=True)  38.5 us
    ppermute x1, starting transfers between devices, shards(): other = by_rows(lax.ppermute(samples, 'core', swap))  8.74 us
    all_to_all x2, starting transfers between devices, exchanged(): return lax.all_to_all(pieces, axis, split_axis=0, concat_axis=0, tiled=True)  7.51 us
    all_to_all x2, waiting for transfers between devices, exchanged(): return lax.all_to_all(pieces, axis, split_axis=0, concat_axis=0, tiled=True)  5.76 us
    ppermute x1, waiting for transfers between devices, shards(): lax.ppermute(jnp.where(first, samples[:EDGE], other[:EDGE]), TM, ahead_ro...  4.71 us
    pallas_call x3, Pallas kernels, call(): pl.pallas_call(kernel, out_shape=[pltpu.VMEM(shape, dtype) for shape, dty...  4.05 us
  transfers between devices with their start and end apart: 4, of which 2 were waited for; matrix products, arithmetic and copies ran while one was open for 1% of the time, Pallas kernels for 2%

profile of v5, /device:TPU:1, one launch (start us, length us, event | category | flops | bytes accessed | tf_op | source)
XLA Modules:
  0.0 74.2 jit_solution(16800502715996716474)
XLA Ops:
  0.0 8.7 %collective-permute-start = (bf16[512,512]{1,0:T(8,128)(2,1)}, bf16[512,512]{1,0:T(8,128)(2,1)S(1)}, u32[]{:S(2)}, u32[]{:S(2)}) collective-permute-start(bf16[512,512]{1,0:T(8,128)(2,1)} %samples_hbm.1), channel_id=1, source_target_pairs={{0,8},{8,0},{1,9},{9,1},{2,10},{10,2},{3,11},{11,3},{4,12},{12,4},... | collective-permute-start | bytes 1572872 | tf_op jit(solution)/shard_map/ppermute | solution.py:160
  8.7 1.8 %shard_map.28 = (f32[520,128]{1,0:T(8,128)S(1)}, bf16[512,512]{1,0:T(8,128)(2,1)S(1)}) custom-call(bf16[512,512]{1,0:T(8,128)(2,1)} %samples_hbm.1, bf16[4,512,256]{2,1,0:T(8,128)(2,1)} %sketch_hbm.1), custom_call_target="tpu_custom_call" | custom-call | tf_op jit(solution)/shard_map/pallas_call | solution.py:27
  10.6 0.0 collective-permute-done.other_ref
  10.6 0.8 %shard_map.29 = f32[1088,128]{1,0:T(8,128)S(1)} custom-call(bf16[512,512]{1,0:T(8,128)(2,1)S(1)} %collective-permute-done.other_ref, bf16[512,512]{1,0:T(8,128)(2,1)S(1)} %get-tuple-element.10.columns_ref, f32[520,128]{1,0:T(8,128)S(1)} %get-tuple-element.11.own_ref), custom_call_target="tpu_custom_call" | custom-call | tf_op jit(solution)/shard_map/pallas_call | solution.py:27
  11.4 0.0 copy-start
  11.4 0.7 convert_element_type.18
  12.1 3.4 %all-to-all-start = ((f16[8,136,128]{2,1,0:T(8,128)(2,1)}), f16[8,136,128]{2,1,0:T(8,128)(2,1)S(1)}, u32[]{:S(2)}, u32[]{:S(2)}) async-start(f16[8,136,128]{2,1,0:T(8,128)(2,1)} %bitcast), calls=%async_computation | async-start | bytes 557056 | tf_op jit(solution)/shard_map/all_to_all | solution.py:43
  15.6 0.2 copy.3
  15.8 0.2 copy.4
  16.0 5.8 %all-to-all-done = f16[8,136,128]{2,1,0:T(8,128)(2,1)S(1)} async-done(((f16[8,136,128]{2,1,0:T(8,128)(2,1)}), f16[8,136,128]{2,1,0:T(8,128)(2,1)S(1)}, u32[]{:S(2)}, u32[]{:S(2)}) %all-to-all-start) | async-done | bytes 278560 | tf_op jit(solution)/shard_map/all_to_all | solution.py:43
  21.8 0.1 fusion.3
  21.9 0.7 broadcast_in_dim.4
  22.6 4.1 %all-to-all-start.1 = ((bf16[8,136,128]{2,1,0:T(8,128)(2,1)}), bf16[8,136,128]{2,1,0:T(8,128)(2,1)S(1)}, u32[]{:S(2)}, u32[]{:S(2)}) async-start(bf16[8,136,128]{2,1,0:T(8,128)(2,1)} %broadcast_in_dim.4), calls=%async_computation.1 | async-start | bytes 557056 | tf_op jit(solution)/shard_map/all_to_all | solution.py:43
  26.7 0.2 copy.5
  26.9 0.2 copy.6
  27.1 1.3 %collective-permute-start.1 = (bf16[8,512]{0,1:T(8,128)(2,1)S(1)}, bf16[8,512]{0,1:T(8,128)(2,1)S(1)}, u32[]{:S(2)}, u32[]{:S(2)}) collective-permute-start(bf16[8,512]{0,1:T(8,128)(2,1)S(1)} %broadcast_select_fusion), channel_id=1, source_target_pairs={{16,0},{24,8},{32,16},{40,24},{48,32},{56,40},{64,48},{72,56},{80,... | collective-permute-start | bytes 24584 | tf_op jit(solution)/shard_map/ppermute | solution.py:170
  28.4 4.7 %collective-permute-done.1 = bf16[8,512]{0,1:T(8,128)(2,1)S(1)} collective-permute-done((bf16[8,512]{0,1:T(8,128)(2,1)S(1)}, bf16[8,512]{0,1:T(8,128)(2,1)S(1)}, u32[]{:S(2)}, u32[]{:S(2)}) %collective-permute-start.1) | collective-permute-done | bytes 8224 | tf_op jit(solution)/shard_map/ppermute | solution.py:170
  33.1 0.0 all-to-all-done.1
  33.2 0.1 bitcast_convert_fusion.sums_ref
  33.2 1.4 %shard_map.30 = f32[512,512]{1,0:T(8,128)S(1)} custom-call(bf16[512,512]{1,0:T(8,128)(2,1)S(1)} %bitcast.13, bf16[512,512]{1,0:T(8,128)(2,1)S(1)} %bitcast.14, bf16[512,128]{1,0:T(8,128)(2,1)S(1)} %pad_bitcast_fusion.tail_ref, f32[1088,128]{1,0:T(8,128)S(1)} %bitcast_convert_fusion.sums_ref), custom_call_target="tpu_custom_call" | custom-call | tf_op jit(solution)/shard_map/pallas_call | solution.py:27
  34.7 0.1 convert_bitcast_fusion
  34.8 38.5 %all_to_all.15 = f16[64,8,512]{2,1,0:T(8,128)(2,1)S(1)} all-to-all(f16[64,8,512]{2,1,0:T(8,128)(2,1)S(1)} %convert_bitcast_fusion), channel_id=1, replica_groups=mesh['y_hi'=4,'z'=8,'core'=2,'y_lo'=2,'x'=4] {'y_hi','z','core'}, dimensions={0} | all-to-all | bytes 1048576 | tf_op jit(solution)/shard_map/all_to_all | solution.py:43
  73.3 0.2 fusion.1
  73.5 0.6 maximum_bitcast_fusion
  (8 shorter events, 0.1 us)
Async XLA Ops:
  0.0 10.6 %collective-permute-start = (bf16[512,512]{1,0:T(8,128)(2,1)}, bf16[512,512]{1,0:T(8,128)(2,1)S(1)}, u32[]{:S(2)}, u32[]{:S(2)}) collective-permute-start(bf16[512,512]{1,0:T(8,128)(2,1)} %samples_hbm.1), channel_id=1, source_target_pairs={{0,8},{8,0},{1,9},{9,1},{2,10},{10,2},{3,11},{11,3},{4,12},{12,4},... | collective-permute-start | bytes 1572872 | tf_op jit(solution)/shard_map/ppermute | solution.py:160
  11.4 4.2 %copy-start = (bf16[512,512]{1,0:T(8,128)(2,1)S(1)}, bf16[512,512]{1,0:T(8,128)(2,1)}, u32[]{:S(2)}) copy-start(bf16[512,512]{1,0:T(8,128)(2,1)} %samples_hbm.1) | copy-start | bytes 1572868
  12.1 9.6 %all-to-all-start = ((f16[8,136,128]{2,1,0:T(8,128)(2,1)}), f16[8,136,128]{2,1,0:T(8,128)(2,1)S(1)}, u32[]{:S(2)}, u32[]{:S(2)}) async-start(f16[8,136,128]{2,1,0:T(8,128)(2,1)} %bitcast), calls=%async_computation | async-start | bytes 557056 | tf_op jit(solution)/shard_map/all_to_all | solution.py:43
  22.6 10.5 %all-to-all-start.1 = ((bf16[8,136,128]{2,1,0:T(8,128)(2,1)}), bf16[8,136,128]{2,1,0:T(8,128)(2,1)S(1)}, u32[]{:S(2)}, u32[]{:S(2)}) async-start(bf16[8,136,128]{2,1,0:T(8,128)(2,1)} %broadcast_in_dim.4), calls=%async_computation.1 | async-start | bytes 557056 | tf_op jit(solution)/shard_map/all_to_all | solution.py:43
  27.1 6.0 %collective-permute-start.1 = (bf16[8,512]{0,1:T(8,128)(2,1)S(1)}, bf16[8,512]{0,1:T(8,128)(2,1)S(1)}, u32[]{:S(2)}, u32[]{:S(2)}) collective-permute-start(bf16[8,512]{0,1:T(8,128)(2,1)S(1)} %broadcast_select_fusion), channel_id=1, source_target_pairs={{16,0},{24,8},{32,16},{40,24},{48,32},{56,40},{64,48},{72,56},{80,... | collective-permute-start | bytes 24584 | tf_op jit(solution)/shard_map/ppermute | solution.py:170

commit v6 on v4

--- a/solution.py
+++ b/solution.py
@@ -16,6 +16,7 @@
 LANES = 128
 SKETCH_ROOT = 512.0
 IMAGE_ROOT = 128.0
+LEAST = 1e-30
 ANY = pl.BlockSpec(memory_space=pl.ANY)
 VMEM = pl.BlockSpec(memory_space=pltpu.VMEM)
 
@@ -44,8 +45,8 @@
 
 
 def coded(values, root_scale):
-    root = jnp.sqrt(jnp.abs(values)) * root_scale
-    return jnp.where(values < 0, -root, root).astype(jnp.float16)
+    root = values * lax.rsqrt(jnp.maximum(jnp.abs(values), LEAST))
+    return (root * root_scale).astype(jnp.float16)
 
 
 def decoded(codes, root_scale):
@@ -184,6 +185,7 @@
     pieces = coded(found, IMAGE_ROOT).reshape(groups, local // groups, blocks * half)
     landed = exchanged(pieces, TM)
     landed = landed.reshape(groups // cores, cores, local // groups, blocks * half)
+    landed = lax.optimization_barrier(landed)
     mine = decoded(landed, IMAGE_ROOT).sum(0).reshape(cores, local // groups, blocks, half)
     return jnp.concatenate([mine[k] for k in range(cores)], -1)[None]
 

time: 74.5 us -> 74 us (level)
  no operation moved by 1% of the time
where the time goes in v6:
time: 74 us; the launch traced here: 73.7 us
  blocking collectives  38.5 us (52%)
  starting transfers between devices  17.6 us (24%)
  waiting for transfers between devices  10.5 us (14%)
  Pallas kernels  3.39 us (5%)
  other arithmetic  2.04 us (3%)
  local copies, waits for them, and re-layouts  1.56 us (2%)
    all_to_all x1, blocking collectives, exchanged(): return lax.all_to_all(pieces, axis, split_axis=0, concat_axis=0, tiled=True)  38.5 us
    ppermute x1, starting transfers between devices, shards(): other = by_rows(lax.ppermute(samples, 'core', swap))  8.74 us
    all_to_all x2, starting transfers between devices, exchanged(): return lax.all_to_all(pieces, axis, split_axis=0, concat_axis=0, tiled=True)  7.52 us
    all_to_all x2, waiting for transfers between devices, exchanged(): return lax.all_to_all(pieces, axis, split_axis=0, concat_axis=0, tiled=True)  5.75 us
    ppermute x1, waiting for transfers between devices, shards(): lax.ppermute(jnp.where(first, samples[:EDGE], other[:EDGE]), TM, ahead_ro...  4.71 us
    pallas_call x3, Pallas kernels, call(): pl.pallas_call(kernel, out_shape=[pltpu.VMEM(shape, dtype) for shape, dty...  3.39 us
  transfers between devices with their start and end apart: 4, of which 2 were waited for; matrix products, arithmetic and copies ran while one was open for 1% of the time, Pallas kernels for 2%

profile of v6, /device:TPU:1, one launch (start us, length us, event | category | flops | bytes accessed | tf_op | source)
XLA Modules:
  0.0 73.7 jit_solution(6872479625278379396)
XLA Ops:
  0.0 8.7 %collective-permute-start = (bf16[512,512]{1,0:T(8,128)(2,1)}, bf16[512,512]{1,0:T(8,128)(2,1)S(1)}, u32[]{:S(2)}, u32[]{:S(2)}) collective-permute-start(bf16[512,512]{1,0:T(8,128)(2,1)} %samples_hbm.1), channel_id=1, source_target_pairs={{0,8},{8,0},{1,9},{9,1},{2,10},{10,2},{3,11},{11,3},{4,12},{12,4},... | collective-permute-start | bytes 1572872 | tf_op jit(solution)/shard_map/ppermute | solution.py:159
  8.7 1.8 %shard_map.28 = (f32[520,128]{1,0:T(8,128)S(1)}, bf16[512,512]{1,0:T(8,128)(2,1)S(1)}) custom-call(bf16[512,512]{1,0:T(8,128)(2,1)} %samples_hbm.1, bf16[4,512,256]{2,1,0:T(8,128)(2,1)} %sketch_hbm.1), custom_call_target="tpu_custom_call" | custom-call | tf_op jit(solution)/shard_map/pallas_call | solution.py:28
  10.6 0.0 collective-permute-done.other_ref
  10.6 0.4 shard_map.29
  11.0 0.0 copy-start
  11.1 0.8 %multiply_convert_fusion.1 = f16[1088,128]{1,0:T(8,128)(2,1)} fusion(f32[1088,128]{1,0:T(8,128)S(1)} %shard_map.29), kind=kLoop, calls=%fused_computation.5 | loop fusion | flops 696320 | bytes 835584 | tf_op jit(solution)/shard_map/convert_element_type | solution.py:49
  11.9 3.4 %all-to-all-start = ((f16[8,136,128]{2,1,0:T(8,128)(2,1)}), f16[8,136,128]{2,1,0:T(8,128)(2,1)S(1)}, u32[]{:S(2)}, u32[]{:S(2)}) async-start(f16[8,136,128]{2,1,0:T(8,128)(2,1)} %bitcast), calls=%async_computation | async-start | bytes 557056 | tf_op jit(solution)/shard_map/all_to_all | solution.py:44
  15.3 0.2 copy.3
  15.5 0.2 copy.4
  15.8 5.7 %all-to-all-done = f16[8,136,128]{2,1,0:T(8,128)(2,1)S(1)} async-done(((f16[8,136,128]{2,1,0:T(8,128)(2,1)}), f16[8,136,128]{2,1,0:T(8,128)(2,1)S(1)}, u32[]{:S(2)}, u32[]{:S(2)}) %all-to-all-start) | async-done | bytes 278560 | tf_op jit(solution)/shard_map/all_to_all | solution.py:44
  21.5 0.1 fusion.1
  21.6 0.7 broadcast_in_dim.4
  22.3 4.1 %all-to-all-start.1 = ((bf16[8,136,128]{2,1,0:T(8,128)(2,1)}), bf16[8,136,128]{2,1,0:T(8,128)(2,1)S(1)}, u32[]{:S(2)}, u32[]{:S(2)}) async-start(bf16[8,136,128]{2,1,0:T(8,128)(2,1)} %broadcast_in_dim.4), calls=%async_computation.1 | async-start | bytes 557056 | tf_op jit(solution)/shard_map/all_to_all | solution.py:44
  26.5 0.2 copy.5
  26.6 0.2 copy.6
  26.8 1.3 %collective-permute-start.1 = (bf16[8,512]{0,1:T(8,128)(2,1)S(1)}, bf16[8,512]{0,1:T(8,128)(2,1)S(1)}, u32[]{:S(2)}, u32[]{:S(2)}) collective-permute-start(bf16[8,512]{0,1:T(8,128)(2,1)S(1)} %broadcast_select_fusion), channel_id=1, source_target_pairs={{16,0},{24,8},{32,16},{40,24},{48,32},{56,40},{64,48},{72,56},{80,... | collective-permute-start | bytes 24584 | tf_op jit(solution)/shard_map/ppermute | solution.py:169
  28.1 4.7 %collective-permute-done.1 = bf16[8,512]{0,1:T(8,128)(2,1)S(1)} collective-permute-done((bf16[8,512]{0,1:T(8,128)(2,1)S(1)}, bf16[8,512]{0,1:T(8,128)(2,1)S(1)}, u32[]{:S(2)}, u32[]{:S(2)}) %collective-permute-start.1) | collective-permute-done | bytes 8224 | tf_op jit(solution)/shard_map/ppermute | solution.py:169
  32.9 0.0 all-to-all-done.1
  32.9 0.1 bitcast_convert_fusion.sums_ref
  33.0 1.1 %shard_map.30 = f32[512,512]{1,0:T(8,128)S(1)} custom-call(bf16[512,512]{1,0:T(8,128)(2,1)S(1)} %bitcast.13, bf16[512,512]{1,0:T(8,128)(2,1)S(1)} %bitcast.14, bf16[512,128]{1,0:T(8,128)(2,1)S(1)} %pad_bitcast_fusion.tail_ref, f32[1088,128]{1,0:T(8,128)S(1)} %bitcast_convert_fusion.sums_ref), custom_call_target="tpu_custom_call" | custom-call | tf_op jit(solution)/shard_map/pallas_call | solution.py:28
  34.1 0.2 fusion.2
  34.3 38.5 %all_to_all.15 = f16[64,8,512]{2,1,0:T(8,128)(2,1)S(1)} all-to-all(f16[64,8,512]{2,1,0:T(8,128)(2,1)S(1)} %fusion.2), channel_id=1, replica_groups=mesh['y_hi'=4,'z'=8,'core'=2,'y_lo'=2,'x'=4] {'y_hi','z','core'}, dimensions={0} | all-to-all | bytes 1048576 | tf_op jit(solution)/shard_map/all_to_all | solution.py:44
  72.8 0.2 fusion
  73.0 0.6 maximum_bitcast_fusion
  (8 shorter events, 0.1 us)
Async XLA Ops:
  0.0 10.6 %collective-permute-start = (bf16[512,512]{1,0:T(8,128)(2,1)}, bf16[512,512]{1,0:T(8,128)(2,1)S(1)}, u32[]{:S(2)}, u32[]{:S(2)}) collective-permute-start(bf16[512,512]{1,0:T(8,128)(2,1)} %samples_hbm.1), channel_id=1, source_target_pairs={{0,8},{8,0},{1,9},{9,1},{2,10},{10,2},{3,11},{11,3},{4,12},{12,4},... | collective-permute-start | bytes 1572872 | tf_op jit(solution)/shard_map/ppermute | solution.py:159
  11.0 4.3 %copy-start = (bf16[512,512]{1,0:T(8,128)(2,1)S(1)}, bf16[512,512]{1,0:T(8,128)(2,1)}, u32[]{:S(2)}) copy-start(bf16[512,512]{1,0:T(8,128)(2,1)} %samples_hbm.1) | copy-start | bytes 1572868
  11.9 9.6 %all-to-all-start = ((f16[8,136,128]{2,1,0:T(8,128)(2,1)}), f16[8,136,128]{2,1,0:T(8,128)(2,1)S(1)}, u32[]{:S(2)}, u32[]{:S(2)}) async-start(f16[8,136,128]{2,1,0:T(8,128)(2,1)} %bitcast), calls=%async_computation | async-start | bytes 557056 | tf_op jit(solution)/shard_map/all_to_all | solution.py:44
  22.3 10.5 %all-to-all-start.1 = ((bf16[8,136,128]{2,1,0:T(8,128)(2,1)}), bf16[8,136,128]{2,1,0:T(8,128)(2,1)S(1)}, u32[]{:S(2)}, u32[]{:S(2)}) async-start(bf16[8,136,128]{2,1,0:T(8,128)(2,1)} %broadcast_in_dim.4), calls=%async_computation.1 | async-start | bytes 557056 | tf_op jit(solution)/shard_map/all_to_all | solution.py:44
  26.8 6.0 %collective-permute-start.1 = (bf16[8,512]{0,1:T(8,128)(2,1)S(1)}, bf16[8,512]{0,1:T(8,128)(2,1)S(1)}, u32[]{:S(2)}, u32[]{:S(2)}) collective-permute-start(bf16[8,512]{0,1:T(8,128)(2,1)S(1)} %broadcast_select_fusion), channel_id=1, source_target_pairs={{16,0},{24,8},{32,16},{40,24},{48,32},{56,40},{64,48},{72,56},{80,... | collective-permute-start | bytes 24584 | tf_op jit(solution)/shard_map/ppermute | solution.py:169

commit v7 on v6

--- a/solution.py
+++ b/solution.py
@@ -13,7 +13,6 @@
 TM = ("y_hi", "z", "core")
 CHAN = ("y_lo", "x")
 EDGE = 8
-LANES = 128
 SKETCH_ROOT = 512.0
 IMAGE_ROOT = 128.0
 LEAST = 1e-30
@@ -126,18 +125,22 @@
     core = lax.axis_index("core")
     mine = pl.ds(pl.multiple_of(core * rows, rows), rows)
     theirs = pl.ds(pl.multiple_of((cores - 1 - core) * rows, rows), rows)
-    ends = pl.ds(cores * rows, tail_ref.shape[1])
+    ends = pl.ds(cores * rows, tail_ref.shape[0])
     depth = cores * rows + 2 * EDGE
     held[:EDGE] = jnp.zeros((EDGE, width), jnp.float32)
     held[EDGE:] = sums_ref[...]
-    steps[depth:] = jnp.zeros((steps.shape[0] - depth, steps.shape[1]), steps.dtype)
     for i in range(block_rows):
         moved = held[EDGE - 1 - i : EDGE - 1 - i + depth]
         steps[:depth, i * width : (i + 1) * width] = moved.astype(steps.dtype)
     wide = 2 * width
     for i in range(0, block_rows * width, wide):
-        found = jnp.zeros((out_ref.shape[0], wide), jnp.float32)
-        for turned, where in ((own_ref, mine), (other_ref, theirs), (tail_ref, ends)):
+        found = lax.dot_general(
+            tail_ref[...],
+            steps[ends, i : i + wide],
+            (((0,), (0,)), ((), ())),
+            preferred_element_type=jnp.float32,
+        )
+        for turned, where in ((own_ref, mine), (other_ref, theirs)):
             found = found + jnp.dot(
                 turned[...], steps[where, i : i + wide], preferred_element_type=jnp.float32
             )
@@ -164,13 +167,16 @@
         [pltpu.VMEM(samples.shape, samples.dtype), held, pltpu.SemaphoreType.DMA((blocks + 2,))],
         in_vmem=False,
     )(samples, sketch)
-    (partial,) = local_kernel(sketched_chip, [((reach, half), jnp.float32)], [held])(other, columns, own)
+    (partial,) = local_kernel(
+        sketched_chip, [((reach, half), jnp.float32)], [held]
+    )(other, columns, own)
     first = lax.axis_index("core") == 0
-    ahead = lax.ppermute(jnp.where(first, samples[:EDGE], other[:EDGE]), TM, ahead_route)
+    edge = jnp.where(first, samples[:EDGE], other[:EDGE])
+    ahead = by_rows(lax.ppermute(edge, TM, ahead_route))
     arrived = exchanged(coded(partial, SKETCH_ROOT).reshape(near, part, half), CHAN)
     total = decoded(arrived, SKETCH_ROOT).sum(0).astype(jnp.bfloat16)
     total, *turned = lax.optimization_barrier((total, samples.T, other.T))
-    tail = jnp.pad(ahead, ((0, LANES - EDGE), (0, 0)))
+    tail = jnp.pad(ahead, ((0, EDGE), (0, 0)))
     sums = exchanged(jnp.broadcast_to(total[None], (near, part, half)), CHAN)
     sums = sums.astype(jnp.float32).reshape(reach, half)
     scale = 1.0 / (rows * groups) ** 0.5
@@ -179,11 +185,13 @@
         [((local, blocks * half), jnp.float32)],
         [
             pltpu.VMEM((EDGE + reach, half), jnp.float32),
-            pltpu.VMEM((cores * rows + LANES, blocks * half), jnp.bfloat16),
+            pltpu.VMEM((cores * rows + 2 * EDGE, blocks * half), jnp.bfloat16),
         ],
-    )(*turned, tail.T, sums)
-    pieces = coded(found, IMAGE_ROOT).reshape(groups, local // groups, blocks * half)
-    landed = exchanged(pieces, TM)
+    )(*turned, tail, sums)
+    high, deep = lax.axis_size("y_hi"), lax.axis_size("z")
+    pieces = coded(found, IMAGE_ROOT).reshape(high, deep, -1, blocks * half)
+    pieces = jnp.swapaxes(pieces, 0, 1).reshape(groups, local // groups, blocks * half)
+    landed = exchanged(pieces, ("z", "y_hi", "core"))
     landed = landed.reshape(groups // cores, cores, local // groups, blocks * half)
     landed = lax.optimization_barrier(landed)
     mine = decoded(landed, IMAGE_ROOT).sum(0).reshape(cores, local // groups, blocks, half)
@@ -194,4 +202,6 @@
     sizes = {"y_hi": 4, "z": 8, "core": 2, "y_lo": 2, "x": 4}
     fine = Mesh(mesh.devices.reshape(tuple(sizes.values())), tuple(sizes))
     placed = (P(TM, CHAN), P(None, CHAN, None))
-    return jax.shard_map(shards, mesh=fine, in_specs=placed, out_specs=P(CHAN, TM, None, None), check_vma=False)
+    return jax.shard_map(
+        shards, mesh=fine, in_specs=placed, out_specs=P(CHAN, TM, None, None), check_vma=False
+    )

time: 74 us -> 71.1 us (0.961)
  the two profiles are of different devices: /device:TPU:1 before, /device:TPU:11 now
where the time goes in v7:
time: 71.1 us; the launch traced here: 70.7 us
  blocking collectives  37.8 us (53%)
  starting transfers between devices  16.9 us (24%)
  waiting for transfers between devices  9.13 us (13%)
  Pallas kernels  3.36 us (5%)
  other arithmetic  2.03 us (3%)
  local copies, waits for them, and re-layouts  1.3 us (2%)
    all_to_all x1, blocking collectives, exchanged(): return lax.all_to_all(pieces, axis, split_axis=0, concat_axis=0, tiled=True)  37.8 us
    all_to_all x2, starting transfers between devices, exchanged(): return lax.all_to_all(pieces, axis, split_axis=0, concat_axis=0, tiled=True)  13.1 us
    all_to_all x2, waiting for transfers between devices, exchanged(): return lax.all_to_all(pieces, axis, split_axis=0, concat_axis=0, tiled=True)  5.74 us
    ppermute x1, waiting for transfers between devices, shards(): ahead = by_rows(lax.ppermute(edge, TM, ahead_route))  3.39 us
    pallas_call x3, Pallas kernels, call(): pl.pallas_call(kernel, out_shape=[pltpu.VMEM(shape, dtype) for shape, dty...  3.36 us
    ppermute x1, starting transfers between devices, shards(): other = by_rows(lax.ppermute(samples, 'core', swap))  2.57 us
  transfers between devices with their start and end apart: 4, of which 2 were waited for; matrix products, arithmetic and copies ran while one was open for 1% of the time, Pallas kernels for 3%

profile of v7, /device:TPU:11, one launch (start us, length us, event | category | flops | bytes accessed | tf_op | source)
XLA Modules:
  0.0 70.7 jit_solution(14359227287620451323)
XLA Ops:
  0.0 2.6 %collective-permute-start = (bf16[512,512]{1,0:T(8,128)(2,1)}, bf16[512,512]{1,0:T(8,128)(2,1)S(1)}, u32[]{:S(2)}, u32[]{:S(2)}) collective-permute-start(bf16[512,512]{1,0:T(8,128)(2,1)} %samples_hbm.1), channel_id=1, source_target_pairs={{0,8},{8,0},{1,9},{9,1},{2,10},{10,2},{3,11},{11,3},{4,12},{12,4},... | collective-permute-start | bytes 1572872 | tf_op jit(solution)/shard_map/ppermute | solution.py:162
  2.6 1.8 %shard_map.28 = (f32[520,128]{1,0:T(8,128)S(1)}, bf16[512,512]{1,0:T(8,128)(2,1)S(1)}) custom-call(bf16[512,512]{1,0:T(8,128)(2,1)} %samples_hbm.1, bf16[4,512,256]{2,1,0:T(8,128)(2,1)} %sketch_hbm.1), custom_call_target="tpu_custom_call" | custom-call | tf_op jit(solution)/shard_map/pallas_call | solution.py:27
  4.4 0.0 collective-permute-done.other_ref
  4.4 0.5 shard_map.29
  4.9 0.0 copy-start
  4.9 0.8 %multiply_convert_fusion.1 = f16[1088,128]{1,0:T(8,128)(2,1)} fusion(f32[1088,128]{1,0:T(8,128)S(1)} %shard_map.29), kind=kLoop, calls=%fused_computation.5 | loop fusion | flops 696320 | bytes 835584 | tf_op jit(solution)/shard_map/convert_element_type | solution.py:48
  5.7 8.8 %all-to-all-start = ((f16[8,136,128]{2,1,0:T(8,128)(2,1)}), f16[8,136,128]{2,1,0:T(8,128)(2,1)S(1)}, u32[]{:S(2)}, u32[]{:S(2)}) async-start(f16[8,136,128]{2,1,0:T(8,128)(2,1)} %bitcast), calls=%async_computation | async-start | bytes 557056 | tf_op jit(solution)/shard_map/all_to_all | solution.py:43
  14.6 0.0 copy-done
  14.6 0.2 copy.5
  14.8 0.2 copy.6
  15.0 5.7 %all-to-all-done = f16[8,136,128]{2,1,0:T(8,128)(2,1)S(1)} async-done(((f16[8,136,128]{2,1,0:T(8,128)(2,1)}), f16[8,136,128]{2,1,0:T(8,128)(2,1)S(1)}, u32[]{:S(2)}, u32[]{:S(2)}) %all-to-all-start) | async-done | bytes 278560 | tf_op jit(solution)/shard_map/all_to_all | solution.py:43
  20.7 0.1 fusion.1
  20.8 0.7 %broadcast_in_dim.4 = bf16[8,136,128]{2,1,0:T(8,128)(2,1)} broadcast(bf16[136,128]{1,0:T(8,128)(2,1)S(1)} %fusion.1), dimensions={1,2} | broadcast | bytes 313344 | tf_op jit(solution)/shard_map/broadcast_in_dim | solution.py:180
  21.5 4.2 %all-to-all-start.1 = ((bf16[8,136,128]{2,1,0:T(8,128)(2,1)}), bf16[8,136,128]{2,1,0:T(8,128)(2,1)S(1)}, u32[]{:S(2)}, u32[]{:S(2)}) async-start(bf16[8,136,128]{2,1,0:T(8,128)(2,1)} %broadcast_in_dim.4), calls=%async_computation.1 | async-start | bytes 557056 | tf_op jit(solution)/shard_map/all_to_all | solution.py:43
  25.8 1.3 %collective-permute-start.1 = (bf16[8,512]{1,0:T(8,128)(2,1)S(1)}, bf16[8,512]{1,0:T(8,128)(2,1)S(1)}, u32[]{:S(2)}, u32[]{:S(2)}) collective-permute-start(bf16[8,512]{1,0:T(8,128)(2,1)S(1)} %slice_select_fusion), channel_id=1, source_target_pairs={{16,0},{24,8},{32,16},{40,24},{48,32},{56,40},{64,48},{72,56},{80,... | collective-permute-start | bytes 24584 | tf_op jit(solution)/shard_map/ppermute | solution.py:175
  27.1 3.4 %collective-permute-done.1 = bf16[8,512]{1,0:T(8,128)(2,1)S(1)} collective-permute-done((bf16[8,512]{1,0:T(8,128)(2,1)S(1)}, bf16[8,512]{1,0:T(8,128)(2,1)S(1)}, u32[]{:S(2)}, u32[]{:S(2)}) %collective-permute-start.1) | collective-permute-done | bytes 8224 | tf_op jit(solution)/shard_map/ppermute | solution.py:175
  30.5 0.0 all-to-all-done.1
  30.5 0.1 bitcast_convert_fusion.sums_ref
  30.6 1.1 %shard_map.30 = f32[512,512]{1,0:T(8,128)S(1)} custom-call(bf16[512,512]{1,0:T(8,128)(2,1)S(1)} %bitcast.13, bf16[512,512]{1,0:T(8,128)(2,1)S(1)} %bitcast.14, bf16[16,512]{1,0:T(8,128)(2,1)S(1)} %pad.4.tail_ref, f32[1088,128]{1,0:T(8,128)S(1)} %bitcast_convert_fusion.sums_ref), custom_call_target="tpu_custom_call" | custom-call | tf_op jit(solution)/shard_map/pallas_call | solution.py:27
  31.6 0.2 multiply_convert_fusion
  31.9 0.1 copy.7
  32.0 37.8 %all_to_all.15 = f16[64,8,512]{2,1,0:T(8,128)(2,1)S(1)} all-to-all(f16[64,8,512]{2,1,0:T(8,128)(2,1)S(1)} %bitcast.16), channel_id=1, replica_groups=mesh['y_hi'=4,'z'=8,'core'=2,'y_lo'=2,'x'=4] {'z','y_hi','core'}, dimensions={0} | all-to-all | bytes 1048576 | tf_op jit(solution)/shard_map/all_to_all | solution.py:43
  69.8 0.2 fusion
  70.0 0.6 maximum_bitcast_fusion
  (5 shorter events, 0.0 us)
Async XLA Ops:
  0.0 4.4 %collective-permute-start = (bf16[512,512]{1,0:T(8,128)(2,1)}, bf16[512,512]{1,0:T(8,128)(2,1)S(1)}, u32[]{:S(2)}, u32[]{:S(2)}) collective-permute-start(bf16[512,512]{1,0:T(8,128)(2,1)} %samples_hbm.1), channel_id=1, source_target_pairs={{0,8},{8,0},{1,9},{9,1},{2,10},{10,2},{3,11},{11,3},{4,12},{12,4},... | collective-permute-start | bytes 1572872 | tf_op jit(solution)/shard_map/ppermute | solution.py:162
  4.9 9.7 %copy-start = (bf16[512,512]{1,0:T(8,128)(2,1)S(1)}, bf16[512,512]{1,0:T(8,128)(2,1)}, u32[]{:S(2)}) copy-start(bf16[512,512]{1,0:T(8,128)(2,1)} %samples_hbm.1) | copy-start | bytes 1572868
  5.7 15.0 %all-to-all-start = ((f16[8,136,128]{2,1,0:T(8,128)(2,1)}), f16[8,136,128]{2,1,0:T(8,128)(2,1)S(1)}, u32[]{:S(2)}, u32[]{:S(2)}) async-start(f16[8,136,128]{2,1,0:T(8,128)(2,1)} %bitcast), calls=%async_computation | async-start | bytes 557056 | tf_op jit(solution)/shard_map/all_to_all | solution.py:43
  21.5 9.0 %all-to-all-start.1 = ((bf16[8,136,128]{2,1,0:T(8,128)(2,1)}), bf16[8,136,128]{2,1,0:T(8,128)(2,1)S(1)}, u32[]{:S(2)}, u32[]{:S(2)}) async-start(bf16[8,136,128]{2,1,0:T(8,128)(2,1)} %broadcast_in_dim.4), calls=%async_computation.1 | async-start | bytes 557056 | tf_op jit(solution)/shard_map/all_to_all | solution.py:43
  25.8 4.7 %collective-permute-start.1 = (bf16[8,512]{1,0:T(8,128)(2,1)S(1)}, bf16[8,512]{1,0:T(8,128)(2,1)S(1)}, u32[]{:S(2)}, u32[]{:S(2)}) collective-permute-start(bf16[8,512]{1,0:T(8,128)(2,1)S(1)} %slice_select_fusion), channel_id=1, source_target_pairs={{16,0},{24,8},{32,16},{40,24},{48,32},{56,40},{64,48},{72,56},{80,... | collective-permute-start | bytes 24584 | tf_op jit(solution)/shard_map/ppermute | solution.py:175

commit v8 on v7

--- a/solution.py
+++ b/solution.py
@@ -12,6 +12,7 @@
 
 TM = ("y_hi", "z", "core")
 CHAN = ("y_lo", "x")
+ACROSS = ("x", "y_lo")
 EDGE = 8
 SKETCH_ROOT = 512.0
 IMAGE_ROOT = 128.0
@@ -173,11 +174,11 @@
     first = lax.axis_index("core") == 0
     edge = jnp.where(first, samples[:EDGE], other[:EDGE])
     ahead = by_rows(lax.ppermute(edge, TM, ahead_route))
-    arrived = exchanged(coded(partial, SKETCH_ROOT).reshape(near, part, half), CHAN)
+    arrived = exchanged(coded(partial, SKETCH_ROOT).reshape(near, part, half), ACROSS)
     total = decoded(arrived, SKETCH_ROOT).sum(0).astype(jnp.bfloat16)
     total, *turned = lax.optimization_barrier((total, samples.T, other.T))
     tail = jnp.pad(ahead, ((0, EDGE), (0, 0)))
-    sums = exchanged(jnp.broadcast_to(total[None], (near, part, half)), CHAN)
+    sums = exchanged(jnp.broadcast_to(total[None], (near, part, half)), ACROSS)
     sums = sums.astype(jnp.float32).reshape(reach, half)
     scale = 1.0 / (rows * groups) ** 0.5
     (found,) = local_kernel(
@@ -188,10 +189,8 @@
             pltpu.VMEM((cores * rows + 2 * EDGE, blocks * half), jnp.bfloat16),
         ],
     )(*turned, tail, sums)
-    high, deep = lax.axis_size("y_hi"), lax.axis_size("z")
-    pieces = coded(found, IMAGE_ROOT).reshape(high, deep, -1, blocks * half)
-    pieces = jnp.swapaxes(pieces, 0, 1).reshape(groups, local // groups, blocks * half)
-    landed = exchanged(pieces, ("z", "y_hi", "core"))
+    pieces = coded(found, IMAGE_ROOT).reshape(groups, local // groups, blocks * half)
+    landed = exchanged(pieces, TM)
     landed = landed.reshape(groups // cores, cores, local // groups, blocks * half)
     landed = lax.optimization_barrier(landed)
     mine = decoded(landed, IMAGE_ROOT).sum(0).reshape(cores, local // groups, blocks, half)

time: 71.1 us -> 70.5 us (level)
  the two profiles are of different devices: /device:TPU:11 before, /device:TPU:1 now
where the time goes in v8:
time: 70.5 us; the launch traced here: 69.6 us
  blocking collectives  34.4 us (49%)
  starting transfers between devices  16.9 us (24%)
  waiting for transfers between devices  11.6 us (16%)
  Pallas kernels  3.35 us (5%)
  other arithmetic  2.03 us (3%)
  local copies, waits for them, and re-layouts  1.2 us (2%)
    all_to_all x1, blocking collectives, exchanged(): return lax.all_to_all(pieces, axis, split_axis=0, concat_axis=0, tiled=True)  34.4 us
    ppermute x1, starting transfers between devices, shards(): other = by_rows(lax.ppermute(samples, 'core', swap))  8.74 us
    all_to_all x2, waiting for transfers between devices, exchanged(): return lax.all_to_all(pieces, axis, split_axis=0, concat_axis=0, tiled=True)  8.24 us
    all_to_all x2, starting transfers between devices, exchanged(): return lax.all_to_all(pieces, axis, split_axis=0, concat_axis=0, tiled=True)  6.83 us
    ppermute x1, waiting for transfers between devices, shards(): ahead = by_rows(lax.ppermute(edge, TM, ahead_route))  3.39 us
    pallas_call x3, Pallas kernels, call(): pl.pallas_call(kernel, out_shape=[pltpu.VMEM(shape, dtype) for shape, dty...  3.35 us
  transfers between devices with their start and end apart: 4, of which 3 were waited for; matrix products, arithmetic and copies ran while one was open for 1% of the time, Pallas kernels for 3%

profile of v8, /device:TPU:1, one launch (start us, length us, event | category | flops | bytes accessed | tf_op | source)
XLA Modules:
  0.0 69.6 jit_solution(13978069572250276604)
XLA Ops:
  0.0 8.7 %collective-permute-start = (bf16[512,512]{1,0:T(8,128)(2,1)}, bf16[512,512]{1,0:T(8,128)(2,1)S(1)}, u32[]{:S(2)}, u32[]{:S(2)}) collective-permute-start(bf16[512,512]{1,0:T(8,128)(2,1)} %samples_hbm.1), channel_id=1, source_target_pairs={{0,8},{8,0},{1,9},{9,1},{2,10},{10,2},{3,11},{11,3},{4,12},{12,4},... | collective-permute-start | bytes 1572872 | tf_op jit(solution)/shard_map/ppermute | solution.py:163
  8.7 1.8 %shard_map.28 = (f32[520,128]{1,0:T(8,128)S(1)}, bf16[512,512]{1,0:T(8,128)(2,1)S(1)}) custom-call(bf16[512,512]{1,0:T(8,128)(2,1)} %samples_hbm.1, bf16[4,512,256]{2,1,0:T(8,128)(2,1)} %sketch_hbm.1), custom_call_target="tpu_custom_call" | custom-call | tf_op jit(solution)/shard_map/pallas_call | solution.py:28
  10.6 0.0 collective-permute-done.other_ref
  10.6 0.4 shard_map.29
  11.0 0.0 copy-start
  11.1 0.8 %multiply_convert_fusion.1 = f16[1088,128]{1,0:T(8,128)(2,1)} fusion(f32[1088,128]{1,0:T(8,128)S(1)} %shard_map.29), kind=kLoop, calls=%fused_computation.5 | loop fusion | flops 696320 | bytes 835584 | tf_op jit(solution)/shard_map/convert_element_type | solution.py:49
  11.9 3.4 %all-to-all-start = ((f16[8,136,128]{2,1,0:T(8,128)(2,1)}), f16[8,136,128]{2,1,0:T(8,128)(2,1)S(1)}, u32[]{:S(2)}, u32[]{:S(2)}) async-start(f16[8,136,128]{2,1,0:T(8,128)(2,1)} %bitcast), calls=%async_computation | async-start | bytes 557056 | tf_op jit(solution)/shard_map/all_to_all | solution.py:44
  15.3 0.0 copy-done
  15.3 0.2 copy.3
  15.5 0.2 copy.4
  15.8 6.8 %all-to-all-done = f16[8,136,128]{2,1,0:T(8,128)(2,1)S(1)} async-done(((f16[8,136,128]{2,1,0:T(8,128)(2,1)}), f16[8,136,128]{2,1,0:T(8,128)(2,1)S(1)}, u32[]{:S(2)}, u32[]{:S(2)}) %all-to-all-start) | async-done | bytes 278560 | tf_op jit(solution)/shard_map/all_to_all | solution.py:44
  22.6 0.1 fusion.1
  22.6 0.7 %broadcast_in_dim.4 = bf16[8,136,128]{2,1,0:T(8,128)(2,1)} broadcast(bf16[136,128]{1,0:T(8,128)(2,1)S(1)} %fusion.1), dimensions={1,2} | broadcast | bytes 313344 | tf_op jit(solution)/shard_map/broadcast_in_dim | solution.py:181
  23.4 3.4 %all-to-all-start.1 = ((bf16[8,136,128]{2,1,0:T(8,128)(2,1)}), bf16[8,136,128]{2,1,0:T(8,128)(2,1)S(1)}, u32[]{:S(2)}, u32[]{:S(2)}) async-start(bf16[8,136,128]{2,1,0:T(8,128)(2,1)} %broadcast_in_dim.4), calls=%async_computation.1 | async-start | bytes 557056 | tf_op jit(solution)/shard_map/all_to_all | solution.py:44
  26.8 1.3 %collective-permute-start.1 = (bf16[8,512]{1,0:T(8,128)(2,1)S(1)}, bf16[8,512]{1,0:T(8,128)(2,1)S(1)}, u32[]{:S(2)}, u32[]{:S(2)}) collective-permute-start(bf16[8,512]{1,0:T(8,128)(2,1)S(1)} %slice_select_fusion), channel_id=1, source_target_pairs={{16,0},{24,8},{32,16},{40,24},{48,32},{56,40},{64,48},{72,56},{80,... | collective-permute-start | bytes 24584 | tf_op jit(solution)/shard_map/ppermute | solution.py:176
  28.1 3.4 %collective-permute-done.1 = bf16[8,512]{1,0:T(8,128)(2,1)S(1)} collective-permute-done((bf16[8,512]{1,0:T(8,128)(2,1)S(1)}, bf16[8,512]{1,0:T(8,128)(2,1)S(1)}, u32[]{:S(2)}, u32[]{:S(2)}) %collective-permute-start.1) | collective-permute-done | bytes 8224 | tf_op jit(solution)/shard_map/ppermute | solution.py:176
  31.5 1.4 %all-to-all-done.1 = bf16[8,136,128]{2,1,0:T(8,128)(2,1)S(1)} async-done(((bf16[8,136,128]{2,1,0:T(8,128)(2,1)}), bf16[8,136,128]{2,1,0:T(8,128)(2,1)S(1)}, u32[]{:S(2)}, u32[]{:S(2)}) %all-to-all-start.1) | async-done | bytes 278560 | tf_op jit(solution)/shard_map/all_to_all | solution.py:44
  33.0 0.1 bitcast_convert_fusion.sums_ref
  33.0 1.1 %shard_map.30 = f32[512,512]{1,0:T(8,128)S(1)} custom-call(bf16[512,512]{1,0:T(8,128)(2,1)S(1)} %bitcast.11, bf16[512,512]{1,0:T(8,128)(2,1)S(1)} %bitcast.12, bf16[16,512]{1,0:T(8,128)(2,1)S(1)} %pad.4.tail_ref, f32[1088,128]{1,0:T(8,128)S(1)} %bitcast_convert_fusion.sums_ref), custom_call_target="tpu_custom_call" | custom-call | tf_op jit(solution)/shard_map/pallas_call | solution.py:28
  34.1 0.2 fusion.2
  34.4 34.4 %all_to_all.15 = f16[64,8,512]{2,1,0:T(8,128)(2,1)S(1)} all-to-all(f16[64,8,512]{2,1,0:T(8,128)(2,1)S(1)} %fusion.2), channel_id=1, replica_groups=mesh['y_hi'=4,'z'=8,'core'=2,'y_lo'=2,'x'=4] {'y_hi','z','core'}, dimensions={0} | all-to-all | bytes 1048576 | tf_op jit(solution)/shard_map/all_to_all | solution.py:44
  68.7 0.2 fusion
  69.0 0.6 maximum_bitcast_fusion
  (5 shorter events, 0.0 us)
Async XLA Ops:
  0.0 10.6 %collective-permute-start = (bf16[512,512]{1,0:T(8,128)(2,1)}, bf16[512,512]{1,0:T(8,128)(2,1)S(1)}, u32[]{:S(2)}, u32[]{:S(2)}) collective-permute-start(bf16[512,512]{1,0:T(8,128)(2,1)} %samples_hbm.1), channel_id=1, source_target_pairs={{0,8},{8,0},{1,9},{9,1},{2,10},{10,2},{3,11},{11,3},{4,12},{12,4},... | collective-permute-start | bytes 1572872 | tf_op jit(solution)/shard_map/ppermute | solution.py:163
  11.0 4.3 %copy-start = (bf16[512,512]{1,0:T(8,128)(2,1)S(1)}, bf16[512,512]{1,0:T(8,128)(2,1)}, u32[]{:S(2)}) copy-start(bf16[512,512]{1,0:T(8,128)(2,1)} %samples_hbm.1) | copy-start | bytes 1572868
  11.9 10.7 %all-to-all-start = ((f16[8,136,128]{2,1,0:T(8,128)(2,1)}), f16[8,136,128]{2,1,0:T(8,128)(2,1)S(1)}, u32[]{:S(2)}, u32[]{:S(2)}) async-start(f16[8,136,128]{2,1,0:T(8,128)(2,1)} %bitcast), calls=%async_computation | async-start | bytes 557056 | tf_op jit(solution)/shard_map/all_to_all | solution.py:44
  23.4 9.6 %all-to-all-start.1 = ((bf16[8,136,128]{2,1,0:T(8,128)(2,1)}), bf16[8,136,128]{2,1,0:T(8,128)(2,1)S(1)}, u32[]{:S(2)}, u32[]{:S(2)}) async-start(bf16[8,136,128]{2,1,0:T(8,128)(2,1)} %broadcast_in_dim.4), calls=%async_computation.1 | async-start | bytes 557056 | tf_op jit(solution)/shard_map/all_to_all | solution.py:44
  26.8 4.7 %collective-permute-start.1 = (bf16[8,512]{1,0:T(8,128)(2,1)S(1)}, bf16[8,512]{1,0:T(8,128)(2,1)S(1)}, u32[]{:S(2)}, u32[]{:S(2)}) collective-permute-start(bf16[8,512]{1,0:T(8,128)(2,1)S(1)} %slice_select_fusion), channel_id=1, source_target_pairs={{16,0},{24,8},{32,16},{40,24},{48,32},{56,40},{64,48},{72,56},{80,... | collective-permute-start | bytes 24584 | tf_op jit(solution)/shard_map/ppermute | solution.py:176

commit v9 on v8

--- a/solution.py
+++ b/solution.py
@@ -12,7 +12,6 @@
 
 TM = ("y_hi", "z", "core")
 CHAN = ("y_lo", "x")
-ACROSS = ("x", "y_lo")
 EDGE = 8
 SKETCH_ROOT = 512.0
 IMAGE_ROOT = 128.0
@@ -133,7 +132,7 @@
     for i in range(block_rows):
         moved = held[EDGE - 1 - i : EDGE - 1 - i + depth]
         steps[:depth, i * width : (i + 1) * width] = moved.astype(steps.dtype)
-    wide = 2 * width
+    wide = block_rows * width
     for i in range(0, block_rows * width, wide):
         found = lax.dot_general(
             tail_ref[...],
@@ -174,11 +173,11 @@
     first = lax.axis_index("core") == 0
     edge = jnp.where(first, samples[:EDGE], other[:EDGE])
     ahead = by_rows(lax.ppermute(edge, TM, ahead_route))
-    arrived = exchanged(coded(partial, SKETCH_ROOT).reshape(near, part, half), ACROSS)
+    arrived = exchanged(coded(partial, SKETCH_ROOT).reshape(near, part, half), CHAN)
     total = decoded(arrived, SKETCH_ROOT).sum(0).astype(jnp.bfloat16)
     total, *turned = lax.optimization_barrier((total, samples.T, other.T))
     tail = jnp.pad(ahead, ((0, EDGE), (0, 0)))
-    sums = exchanged(jnp.broadcast_to(total[None], (near, part, half)), ACROSS)
+    sums = exchanged(jnp.broadcast_to(total[None], (near, part, half)), CHAN)
     sums = sums.astype(jnp.float32).reshape(reach, half)
     scale = 1.0 / (rows * groups) ** 0.5
     (found,) = local_kernel(

time: 70.5 us -> 70.4 us (level)
  waiting for transfers between devices: 11.6 us -> 10.6 us
    all_to_all x2, waiting for transfers between devices: 8.24 us -> 7.22 us  [exchanged(): return lax.all_to_all(pieces, axis, split_axis=0, concat_axis=0, tiled=True)]
where the time goes in v9:
time: 70.4 us; the launch traced here: 69.5 us
  blocking collectives  34.6 us (49%)
  starting transfers between devices  17.6 us (25%)
  waiting for transfers between devices  10.6 us (15%)
  Pallas kernels  3.35 us (5%)
  other arithmetic  2.03 us (3%)
  local copies, waits for them, and re-layouts  1.2 us (2%)
    all_to_all x1, blocking collectives, exchanged(): return lax.all_to_all(pieces, axis, split_axis=0, concat_axis=0, tiled=True)  34.6 us
    ppermute x1, starting transfers between devices, shards(): other = by_rows(lax.ppermute(samples, 'core', swap))  8.74 us
    all_to_all x2, starting transfers between devices, exchanged(): return lax.all_to_all(pieces, axis, split_axis=0, concat_axis=0, tiled=True)  7.52 us
    all_to_all x2, waiting for transfers between devices, exchanged(): return lax.all_to_all(pieces, axis, split_axis=0, concat_axis=0, tiled=True)  7.22 us
    ppermute x1, waiting for transfers between devices, shards(): ahead = by_rows(lax.ppermute(edge, TM, ahead_route))  3.39 us
    pallas_call x3, Pallas kernels, call(): pl.pallas_call(kernel, out_shape=[pltpu.VMEM(shape, dtype) for shape, dty...  3.35 us
  transfers between devices with their start and end apart: 4, of which 3 were waited for; matrix products, arithmetic and copies ran while one was open for 1% of the time, Pallas kernels for 3%

profile of v9, /device:TPU:1, one launch (start us, length us, event | category | flops | bytes accessed | tf_op | source)
XLA Modules:
  0.0 69.5 jit_solution(13374149122872263651)
XLA Ops:
  0.0 8.7 %collective-permute-start = (bf16[512,512]{1,0:T(8,128)(2,1)}, bf16[512,512]{1,0:T(8,128)(2,1)S(1)}, u32[]{:S(2)}, u32[]{:S(2)}) collective-permute-start(bf16[512,512]{1,0:T(8,128)(2,1)} %samples_hbm.1), channel_id=1, source_target_pairs={{0,8},{8,0},{1,9},{9,1},{2,10},{10,2},{3,11},{11,3},{4,12},{12,4},... | collective-permute-start | bytes 1572872 | tf_op jit(solution)/shard_map/ppermute | solution.py:162
  8.7 1.8 %shard_map.28 = (f32[520,128]{1,0:T(8,128)S(1)}, bf16[512,512]{1,0:T(8,128)(2,1)S(1)}) custom-call(bf16[512,512]{1,0:T(8,128)(2,1)} %samples_hbm.1, bf16[4,512,256]{2,1,0:T(8,128)(2,1)} %sketch_hbm.1), custom_call_target="tpu_custom_call" | custom-call | tf_op jit(solution)/shard_map/pallas_call | solution.py:27
  10.6 0.0 collective-permute-done.other_ref
  10.6 0.4 shard_map.29
  11.0 0.0 copy-start
  11.1 0.8 %multiply_convert_fusion.1 = f16[1088,128]{1,0:T(8,128)(2,1)} fusion(f32[1088,128]{1,0:T(8,128)S(1)} %shard_map.29), kind=kLoop, calls=%fused_computation.5 | loop fusion | flops 696320 | bytes 835584 | tf_op jit(solution)/shard_map/convert_element_type | solution.py:48
  11.9 3.4 %all-to-all-start = ((f16[8,136,128]{2,1,0:T(8,128)(2,1)}), f16[8,136,128]{2,1,0:T(8,128)(2,1)S(1)}, u32[]{:S(2)}, u32[]{:S(2)}) async-start(f16[8,136,128]{2,1,0:T(8,128)(2,1)} %bitcast), calls=%async_computation | async-start | bytes 557056 | tf_op jit(solution)/shard_map/all_to_all | solution.py:43
  15.3 0.0 copy-done
  15.3 0.2 copy.3
  15.5 0.2 copy.4
  15.8 5.7 %all-to-all-done = f16[8,136,128]{2,1,0:T(8,128)(2,1)S(1)} async-done(((f16[8,136,128]{2,1,0:T(8,128)(2,1)}), f16[8,136,128]{2,1,0:T(8,128)(2,1)S(1)}, u32[]{:S(2)}, u32[]{:S(2)}) %all-to-all-start) | async-done | bytes 278560 | tf_op jit(solution)/shard_map/all_to_all | solution.py:43
  21.5 0.1 fusion.1
  21.6 0.7 %broadcast_in_dim.4 = bf16[8,136,128]{2,1,0:T(8,128)(2,1)} broadcast(bf16[136,128]{1,0:T(8,128)(2,1)S(1)} %fusion.1), dimensions={1,2} | broadcast | bytes 313344 | tf_op jit(solution)/shard_map/broadcast_in_dim | solution.py:180
  22.3 4.1 %all-to-all-start.1 = ((bf16[8,136,128]{2,1,0:T(8,128)(2,1)}), bf16[8,136,128]{2,1,0:T(8,128)(2,1)S(1)}, u32[]{:S(2)}, u32[]{:S(2)}) async-start(bf16[8,136,128]{2,1,0:T(8,128)(2,1)} %broadcast_in_dim.4), calls=%async_computation.1 | async-start | bytes 557056 | tf_op jit(solution)/shard_map/all_to_all | solution.py:43
  26.5 1.3 %collective-permute-start.1 = (bf16[8,512]{1,0:T(8,128)(2,1)S(1)}, bf16[8,512]{1,0:T(8,128)(2,1)S(1)}, u32[]{:S(2)}, u32[]{:S(2)}) collective-permute-start(bf16[8,512]{1,0:T(8,128)(2,1)S(1)} %slice_select_fusion), channel_id=1, source_target_pairs={{16,0},{24,8},{32,16},{40,24},{48,32},{56,40},{64,48},{72,56},{80,... | collective-permute-start | bytes 24584 | tf_op jit(solution)/shard_map/ppermute | solution.py:175
  27.8 3.4 %collective-permute-done.1 = bf16[8,512]{1,0:T(8,128)(2,1)S(1)} collective-permute-done((bf16[8,512]{1,0:T(8,128)(2,1)S(1)}, bf16[8,512]{1,0:T(8,128)(2,1)S(1)}, u32[]{:S(2)}, u32[]{:S(2)}) %collective-permute-start.1) | collective-permute-done | bytes 8224 | tf_op jit(solution)/shard_map/ppermute | solution.py:175
  31.2 1.5 %all-to-all-done.1 = bf16[8,136,128]{2,1,0:T(8,128)(2,1)S(1)} async-done(((bf16[8,136,128]{2,1,0:T(8,128)(2,1)}), bf16[8,136,128]{2,1,0:T(8,128)(2,1)S(1)}, u32[]{:S(2)}, u32[]{:S(2)}) %all-to-all-start.1) | async-done | bytes 278560 | tf_op jit(solution)/shard_map/all_to_all | solution.py:43
  32.6 0.1 bitcast_convert_fusion.sums_ref
  32.7 1.1 %shard_map.30 = f32[512,512]{1,0:T(8,128)S(1)} custom-call(bf16[512,512]{1,0:T(8,128)(2,1)S(1)} %bitcast.11, bf16[512,512]{1,0:T(8,128)(2,1)S(1)} %bitcast.12, bf16[16,512]{1,0:T(8,128)(2,1)S(1)} %pad.4.tail_ref, f32[1088,128]{1,0:T(8,128)S(1)} %bitcast_convert_fusion.sums_ref), custom_call_target="tpu_custom_call" | custom-call | tf_op jit(solution)/shard_map/pallas_call | solution.py:27
  33.8 0.2 fusion.2
  34.0 34.6 %all_to_all.15 = f16[64,8,512]{2,1,0:T(8,128)(2,1)S(1)} all-to-all(f16[64,8,512]{2,1,0:T(8,128)(2,1)S(1)} %fusion.2), channel_id=1, replica_groups=mesh['y_hi'=4,'z'=8,'core'=2,'y_lo'=2,'x'=4] {'y_hi','z','core'}, dimensions={0} | all-to-all | bytes 1048576 | tf_op jit(solution)/shard_map/all_to_all | solution.py:43
  68.6 0.2 fusion
  68.9 0.6 maximum_bitcast_fusion
  (5 shorter events, 0.0 us)
Async XLA Ops:
  0.0 10.6 %collective-permute-start = (bf16[512,512]{1,0:T(8,128)(2,1)}, bf16[512,512]{1,0:T(8,128)(2,1)S(1)}, u32[]{:S(2)}, u32[]{:S(2)}) collective-permute-start(bf16[512,512]{1,0:T(8,128)(2,1)} %samples_hbm.1), channel_id=1, source_target_pairs={{0,8},{8,0},{1,9},{9,1},{2,10},{10,2},{3,11},{11,3},{4,12},{12,4},... | collective-permute-start | bytes 1572872 | tf_op jit(solution)/shard_map/ppermute | solution.py:162
  11.0 4.3 %copy-start = (bf16[512,512]{1,0:T(8,128)(2,1)S(1)}, bf16[512,512]{1,0:T(8,128)(2,1)}, u32[]{:S(2)}) copy-start(bf16[512,512]{1,0:T(8,128)(2,1)} %samples_hbm.1) | copy-start | bytes 1572868
  11.9 9.6 %all-to-all-start = ((f16[8,136,128]{2,1,0:T(8,128)(2,1)}), f16[8,136,128]{2,1,0:T(8,128)(2,1)S(1)}, u32[]{:S(2)}, u32[]{:S(2)}) async-start(f16[8,136,128]{2,1,0:T(8,128)(2,1)} %bitcast), calls=%async_computation | async-start | bytes 557056 | tf_op jit(solution)/shard_map/all_to_all | solution.py:43
  22.3 10.3 %all-to-all-start.1 = ((bf16[8,136,128]{2,1,0:T(8,128)(2,1)}), bf16[8,136,128]{2,1,0:T(8,128)(2,1)S(1)}, u32[]{:S(2)}, u32[]{:S(2)}) async-start(bf16[8,136,128]{2,1,0:T(8,128)(2,1)} %broadcast_in_dim.4), calls=%async_computation.1 | async-start | bytes 557056 | tf_op jit(solution)/shard_map/all_to_all | solution.py:43
  26.5 4.7 %collective-permute-start.1 = (bf16[8,512]{1,0:T(8,128)(2,1)S(1)}, bf16[8,512]{1,0:T(8,128)(2,1)S(1)}, u32[]{:S(2)}, u32[]{:S(2)}) collective-permute-start(bf16[8,512]{1,0:T(8,128)(2,1)S(1)} %slice_select_fusion), channel_id=1, source_target_pairs={{16,0},{24,8},{32,16},{40,24},{48,32},{56,40},{64,48},{72,56},{80,... | collective-permute-start | bytes 24584 | tf_op jit(solution)/shard_map/ppermute | solution.py:175
